TPU v7x, 32 devices: a whole 2x2x4 slice. The times are simulated.
32 devices in a mesh: atm: 8 (over y, x, core), ocn: 4 (over z).
Axes of the slice: x: 2, y: 2, z: 4, core: 2. Of those that a mesh axis runs over, the one named last changes fastest.
Arguments:
- prior_states: bfloat16 [256, 8, 256], P(('atm', 'ocn')), may hold values from -6 to 6
- patch_mesh_location: int32 [256], P(('atm', 'ocn')), may hold values from 0 to 65535
- fetched_blocks: int32 [256, 5], P(('atm', 'ocn')), may hold values from 0 to 31, all different within a row; in each aligned block of 8 rows (0 to 7, 8 to 15, ...) at most 2 rows name the same one
- measured_deviations: bfloat16 [16384, 256], P(('atm', 'ocn')), may hold values from -6 to 6
- departure_vectors: float32 [16384, 256], P(('atm', 'ocn')), may hold values from -16 to 16
- measurement_error_spread: float32 [16384], P(('atm', 'ocn')), may hold values from 4 to 8
- measurement_mesh_location: int32 [16384], P(('atm', 'ocn')), may hold values from 0 to 65535
Outputs:
- analysis: float32 [256, 8, 256], P(('atm', 'ocn'))
Inputs may be any that keep to these rules, and one draw needn't show every extreme that they name: `fetched_blocks`: each tile names 5 different blocks; among the tiles of one device no block is named by more than 2 tiles, and some block is named by exactly 2 of them.
All inputs are finite; a program needn't handle non-finite values.
Results may differ from a plain program's by a relative error of at most 0.00055.
The roundings to bfloat16 on the way count: a program that leaves them out, or rounds other values in their place, can miss the bound.
Values may be sent and summed in bfloat16 or wider, within the bound.
No kernel may reach another device: no remote copies, remote signals or barrier semaphores. Data moves between devices by JAX's collectives and lax.ppermute only.
A program may use at most 64 MiB of HBM per device.

v0:
```python
import jax
import jax.numpy as jnp
from jax import lax
from jax.sharding import PartitionSpec as P

OBS_BLOCK = 512
READS = 5
CAP = 2
SWEEPS = 2
LENGTH = 16384


def with_halo(shard, sides, width):
    for axis, dim in sides:
        peers, length = (lax.axis_size(axis), shard.shape[dim])
        up = [(i, (i + 1) % peers) for i in range(peers - 1)]
        down = [(j, i) for i, j in up]
        last = lax.slice_in_dim(shard, length - width, length, axis=dim)
        initial = lax.slice_in_dim(shard, 0, width, axis=dim)
        before = lax.ppermute(last, axis, up)
        after = lax.ppermute(initial, axis, down)
        shard = jnp.concatenate([before, shard, after], axis=dim)
    return shard


def taper(first, second):
    spread = (first - second).astype(jnp.float32) / LENGTH
    return 1.0 / (1.0 + spread * spread)


def shards(
    prior_states,
    patch_mesh_location,
    fetched_blocks,
    measured_deviations,
    departure_vectors,
    measurement_error_spread,
    measurement_mesh_location,
):
    housed_patches = prior_states.shape[0]
    patch_lines = prior_states.shape[1]
    sampled_trajectories = prior_states.shape[2]
    inverse = 1.0 / (sampled_trajectories - 1)
    local_blocks = measured_deviations.shape[0] // OBS_BLOCK
    devices = lax.axis_size("atm") * lax.axis_size("ocn")
    nblocks = local_blocks * devices
    padded_y = with_halo(measured_deviations, ((("atm", "ocn"), 0),), OBS_BLOCK)
    padded_q = with_halo(measurement_mesh_location, ((("atm", "ocn"), 0),), OBS_BLOCK)

    def tapered_cross(index):
        product = jnp.einsum(
            "im,jm->ij", measured_deviations, padded_y, preferred_element_type=jnp.float32
        )
        return product * inverse * taper(measurement_mesh_location[:, None], padded_q[None, :])

    tapered = lax.map(tapered_cross, jnp.arange(local_blocks, dtype=jnp.int32))
    own_y = measured_deviations.reshape(local_blocks, OBS_BLOCK, sampled_trajectories)
    own_q = measurement_mesh_location.reshape(local_blocks, OBS_BLOCK)
    floats_y = own_y.astype(jnp.float32)
    diagonal = jnp.sum(floats_y * floats_y, axis=2) * inverse
    target = departure_vectors.reshape(local_blocks, OBS_BLOCK, sampled_trajectories)
    errors = measurement_error_spread.reshape(local_blocks, OBS_BLOCK, 1)
    divisor = diagonal[:, :, None] + errors
    weights = target / divisor
    for repeat in range(SWEEPS):
        padded_w = with_halo(
            weights.reshape(local_blocks * OBS_BLOCK, sampled_trajectories),
            ((("atm", "ocn"), 0),),
            OBS_BLOCK,
        )
        near_w = jnp.stack([padded_w])
        applied = jnp.einsum(
            "bij,bjm->bim",
            tapered,
            near_w,
            precision=lax.Precision.HIGHEST,
            preferred_element_type=jnp.float32,
        )
        applied = applied + errors * weights
        weights = weights + (target - applied) / divisor
    weight_rows = weights.astype(jnp.bfloat16)
    element_numbers = prior_states.astype(jnp.float32)
    anomalies = (element_numbers - jnp.mean(element_numbers, axis=2, keepdims=True)).astype(
        jnp.bfloat16
    )
    chosen = jnp.sum(
        (fetched_blocks[:, :, None] == jnp.arange(nblocks, dtype=jnp.int32)[None, None, :]).astype(
            jnp.int32
        ),
        axis=1,
    )
    before = jnp.cumsum(chosen, axis=0) - chosen
    matched = chosen[:, :, None] * (
        before[:, :, None] == jnp.arange(CAP, dtype=jnp.int32)[None, None, :]
    ).astype(jnp.int32)
    filled = jnp.sum(matched, axis=0).reshape(nblocks * CAP)
    source = jnp.sum(
        matched * jnp.arange(housed_patches, dtype=jnp.int32)[:, None, None], axis=0
    ).reshape(nblocks * CAP)
    send_rows = jnp.take(anomalies, source, axis=0) * filled.astype(jnp.bfloat16)[:, None, None]
    send_rows = send_rows.reshape(devices, local_blocks, CAP, patch_lines, sampled_trajectories)
    places = (jnp.take(patch_mesh_location, source) * filled).reshape(devices, local_blocks, CAP)
    arrived = lax.all_to_all(send_rows, ("atm", "ocn"), split_axis=0, concat_axis=0, tiled=True)
    arrived_places = lax.all_to_all(places, ("atm", "ocn"), split_axis=0, concat_axis=0, tiled=True)
    sources = arrived.shape[0]
    groups = sources // 8

    def group_gain(inputs):
        portion, portion_places = inputs
        product = jnp.einsum("gokrm,ojm->gokrj", portion, own_y, preferred_element_type=jnp.float32)
        weighting = taper(portion_places[:, :, :, None, None], own_q[None, :, None, None, :])
        gain = (product * inverse * weighting).astype(jnp.bfloat16)
        return jnp.einsum("gokrj,ojm->gokrm", gain, weight_rows, preferred_element_type=jnp.float32)

    result = lax.map(
        group_gain,
        (
            arrived.reshape((groups, 8) + arrived.shape[1:]),
            arrived_places.reshape((groups, 8) + arrived_places.shape[1:]),
        ),
    )
    answers = result.reshape(arrived.shape[:3] + (arrived.shape[3], sampled_trajectories))
    returned = lax.all_to_all(answers, ("atm", "ocn"), split_axis=0, concat_axis=0, tiled=True)
    returned = returned.reshape(nblocks * CAP, patch_lines, sampled_trajectories)
    slot_index = fetched_blocks * CAP + jnp.take_along_axis(before, fetched_blocks, axis=1)
    increment = jnp.take(returned, slot_index.reshape(-1), axis=0).reshape(
        housed_patches, READS, patch_lines, sampled_trajectories
    )
    return element_numbers + jnp.sum(increment, axis=1)


def solution(mesh):
    placed = (
        P(("atm", "ocn"), None, None),
        P(("atm", "ocn")),
        P(("atm", "ocn"), None),
        P(("atm", "ocn"), None),
        P(("atm", "ocn"), None),
        P(("atm", "ocn")),
        P(("atm", "ocn")),
    )
    return jax.shard_map(
        shards, mesh=mesh, in_specs=placed, out_specs=P(("atm", "ocn"), None, None), check_vma=False
    )
```

profile of v0, /device:TPU:1, one launch (start us, length us, event | category | flops | bytes accessed | tf_op | source)
XLA Modules:
  0.0 134.2 jit_solution(14241883993466998729)
XLA Ops:
  0.0 4.0 %collective-permute-start = (bf16[512,256]{1,0:T(8,128)(2,1)}, bf16[512,256]{1,0:T(8,128)(2,1)S(1)}, u32[]{:S(2)}, u32[]{:S(2)}) collective-permute-start(bf16[512,256]{1,0:T(8,128)(2,1)} %param.12), channel_id=1, source_target_pairs={{0,1},{1,2},{2,3},{3,4},{4,5},{5,6},{6,7},{7,8},{8,9},{9,10},{10,1... | collective-permute-start | bytes 786440 | tf_op jit(solution)/shard_map/ppermute | solution.py:20
  4.0 4.5 %collective-permute-start.1 = (bf16[512,256]{1,0:T(8,128)(2,1)}, bf16[512,256]{1,0:T(8,128)(2,1)}, u32[]{:S(2)}, u32[]{:S(2)}) collective-permute-start(bf16[512,256]{1,0:T(8,128)(2,1)} %param.12), channel_id=1, source_target_pairs={{1,0},{2,1},{3,2},{4,3},{5,4},{6,5},{7,6},{8,7},{9,8},{10,9},{11,1... | collective-permute-start | bytes 786440 | tf_op jit(solution)/shard_map/ppermute | solution.py:21
  8.5 1.9 %collective-permute-start.2 = (s32[512]{0:T(512)}, s32[512]{0:T(512)S(1)}, u32[]{:S(2)}, u32[]{:S(2)}) collective-permute-start(s32[512]{0:T(512)} %param.15), channel_id=1, source_target_pairs={{0,1},{1,2},{2,3},{3,4},{4,5},{5,6},{6,7},{7,8},{8,9},{9,10},{10,1... | collective-permute-start | bytes 6152 | tf_op jit(solution)/shard_map/ppermute | solution.py:20
  10.5 5.4 %collective-permute-start.3 = (s32[512]{0:T(512)}, s32[512]{0:T(512)S(1)}, u32[]{:S(2)}, u32[]{:S(2)}) collective-permute-start(s32[512]{0:T(512)} %param.15), channel_id=1, source_target_pairs={{1,0},{2,1},{3,2},{4,3},{5,4},{6,5},{7,6},{8,7},{9,8},{10,9},{11,1... | collective-permute-start | bytes 6152 | tf_op jit(solution)/shard_map/ppermute | solution.py:21
  15.9 0.8 copy.40
  16.7 0.1 convert_reduce_fusion.1
  16.8 0.1 copy.42
  16.9 0.1 reshape.260
  17.0 1.6 %fusion.71 = (s32[1]{0:T(128)}, s32[1]{0:T(128)}, s32[1]{0:T(128)}, s32[1]{0:T(128)}, s32[1]{0:T(128)}, /*index=5*/s32[1]{0:T(128)}, s32[1]{0:T(128)}, s32[1]{0:T(128)}) fusion(s32[8]{0:T(128)} %param.10), kind=kLoop, calls=%fused_computation.90 | loop fusion | bytes 64 | tf_op jit(solution)/shard_map/jit(_take)/gather | solution.py:102
  18.7 5.0 %compare_select_fusion.6 = s32[64]{0:T(128)S(1)} fusion(s32[]{:T(128)} %bitcast.23, s32[]{:T(128)} %bitcast.24, s32[]{:T(128)} %bitcast.25, s32[]{:T(128)} %bitcast.26, s32[]{:T(128)} %bitcast.27, s32[]{:T(128)} %bitcast.28, s32[]{:T(128)} %bitcast.29, s32[]{:T(128)} %bitcast.30, s32[64,1]{0,1:T(1,128)S(1)} %reshape.260), kind=kLoop, calls=%fused_computation.75 | loop fusion | flops 1088 | bytes 544 | tf_op jit(solution)/shard_map/jit(_take)/gather | solution.py:102
  23.6 0.1 gather.26
  23.7 0.1 copy.44
  23.8 0.7 copy.45
  24.5 5.5 %all-to-all-start.1 = ((s32[32,1,2]{2,1,0:T(1,128)}), s32[32,1,2]{2,1,0:T(1,128)S(1)}, u32[]{:S(2)}, u32[]{:S(2)}) async-start(s32[32,1,2]{2,1,0:T(1,128)} %copy.45), calls=%async_computation.1 | async-start | bytes 32768 | tf_op jit(solution)/shard_map/all_to_all | solution.py:104
  30.1 1.1 multiply_reduce_fusion
  31.2 0.7 multiply_add_fusion
  31.9 1.2 broadcast_divide_fusion
  33.1 3.3 %collective-permute-start.4 = (f32[512,256]{1,0:T(8,128)S(1)}, f32[512,256]{1,0:T(8,128)S(1)}, u32[]{:S(2)}, u32[]{:S(2)}) collective-permute-start(f32[512,256]{1,0:T(8,128)S(1)} %broadcast_divide_fusion), channel_id=1, source_target_pairs={{0,1},{1,2},{2,3},{3,4},{4,5},{5,6},{6,7},{7,8},{8,9},{9,10},{10,1... | collective-permute-start | bytes 1572872 | tf_op jit(solution)/shard_map/ppermute | solution.py:20
  36.3 0.8 convert_reduce_fusion
  37.2 0.8 fusion.63
  38.0 0.0 collective-permute-done.2
  38.0 4.1 %collective-permute-start.5 = (f32[512,256]{1,0:T(8,128)S(1)}, f32[512,256]{1,0:T(8,128)S(1)}, u32[]{:S(2)}, u32[]{:S(2)}) collective-permute-start(f32[512,256]{1,0:T(8,128)S(1)} %broadcast_divide_fusion), channel_id=1, source_target_pairs={{1,0},{2,1},{3,2},{4,3},{5,4},{6,5},{7,6},{8,7},{9,8},{10,9},{11,1... | collective-permute-start | bytes 1572872 | tf_op jit(solution)/shard_map/ppermute | solution.py:21
  42.2 0.0 collective-permute-done.3
  42.2 0.7 pad_add_fusion
  42.9 0.0 collective-permute-done
  42.9 0.7 copy-done.6
  43.6 0.0 collective-permute-done.1
  43.6 2.7 %fusion.15 = f32[512,1536]{0,1:T(8,128)S(1)} fusion(bf16[512,256]{1,0:T(8,128)(2,1)} %param.12, s32[1536]{0:T(1024)S(1)} %pad_add_fusion, s32[512]{0:T(512)} %param.15, bf16[512,256]{1,0:T(8,128)(2,1)} %collective-permute-done.1, bf16[512,256]{1,0:T(8,128)(2,1)} %copy-done.6), kind=kOutput, calls=%fused_computation.19 | convolution fusion | flops 411303936 | bytes 3940352 | tf_op jit(solution)/shard_map/while/body/eval_jaxpr/im,jm->ij/dot_general | solution.py:51
  46.2 4.1 %collective-permute-done.4 = f32[512,256]{1,0:T(8,128)S(1)} collective-permute-done((f32[512,256]{1,0:T(8,128)S(1)}, f32[512,256]{1,0:T(8,128)S(1)}, u32[]{:S(2)}, u32[]{:S(2)}) %collective-permute-start.4) | collective-permute-done | bytes 524320 | tf_op jit(solution)/shard_map/ppermute | solution.py:20
  50.3 12.1 %collective-permute-done.5 = f32[512,256]{1,0:T(8,128)S(1)} collective-permute-done((f32[512,256]{1,0:T(8,128)S(1)}, f32[512,256]{1,0:T(8,128)S(1)}, u32[]{:S(2)}, u32[]{:S(2)}) %collective-permute-start.5) | collective-permute-done | bytes 524320 | tf_op jit(solution)/shard_map/ppermute | solution.py:21
  62.4 6.1 %fusion.43 = f32[512,256]{1,0:T(8,128)} fusion(f32[512,256]{1,0:T(8,128)S(1)} %broadcast_divide_fusion, f32[512,256]{1,0:T(8,128)S(1)} %copy-done.1, f32[512,1536]{0,1:T(8,128)S(1)} %fusion.15, f32[512,256]{1,0:T(8,128)S(1)} %collective-permute-done.5, f32[512,256]{1,0:T(8,128)S(1)} %collective-permute-done.4, f32[512]{0:T(512)S(1)} %copy-done.5, ...), kind=kOutput, calls=%fused_computation.37 | convolution fusion | flops 2417360896 | bytes 5771264 | tf_op jit(solution)/shard_map/bij,bjm->bim/dot_general | solution.py:72
  68.5 2.2 %collective-permute-start.6 = (f32[512,256]{1,0:T(8,128)}, f32[512,256]{1,0:T(8,128)}, u32[]{:S(2)}, u32[]{:S(2)}) collective-permute-start(f32[512,256]{1,0:T(8,128)} %fusion.43), channel_id=1, source_target_pairs={{0,1},{1,2},{2,3},{3,4},{4,5},{5,6},{6,7},{7,8},{8,9},{9,10},{10,1... | collective-permute-start | bytes 1572872 | tf_op jit(solution)/shard_map/ppermute | solution.py:20
  70.7 5.2 %collective-permute-start.7 = (f32[512,256]{1,0:T(8,128)}, f32[512,256]{1,0:T(8,128)}, u32[]{:S(2)}, u32[]{:S(2)}) collective-permute-start(f32[512,256]{1,0:T(8,128)} %fusion.43), channel_id=1, source_target_pairs={{1,0},{2,1},{3,2},{4,3},{5,4},{6,5},{7,6},{8,7},{9,8},{10,9},{11,1... | collective-permute-start | bytes 1572872 | tf_op jit(solution)/shard_map/ppermute | solution.py:21
  75.9 0.1 copy.41
  76.0 0.1 copy.43
  76.1 1.3 gather_fusion
  77.4 1.8 %select_multiply_fusion = bf16[32,1,2,8,256]{4,3,2,1,0:T(8,128)(2,1)} fusion(bf16[32,1,2,8,256]{4,3,2,1,0:T(8,128)(2,1)} %bitcast.106, pred[32,2]{1,0:T(8,128)(4,1)S(1)} %copy.41, bf16[32,2]{1,0:T(8,128)(2,1)S(1)} %copy.43), kind=kLoop, calls=%fused_computation.50 | loop fusion | flops 262144 | bytes 524480 | tf_op jit(solution)/shard_map/mul | solution.py:100
  79.2 0.0 all-to-all-done.1
  79.2 4.1 %all-to-all-start = ((bf16[32,1,2,8,256]{4,3,2,1,0:T(8,128)(2,1)}), bf16[32,1,2,8,256]{4,3,2,1,0:T(8,128)(2,1)}, u32[]{:S(2)}, u32[]{:S(2)}) async-start(bf16[32,1,2,8,256]{4,3,2,1,0:T(8,128)(2,1)} %select_multiply_fusion), calls=%async_computation | async-start | bytes 524288 | tf_op jit(solution)/shard_map/all_to_all | solution.py:103
  83.3 0.0 copy-start
  83.3 0.0 copy-start.3
  83.4 0.1 copy.48
  83.5 2.5 %collective-permute-done.6 = f32[512,256]{1,0:T(8,128)} collective-permute-done((f32[512,256]{1,0:T(8,128)}, f32[512,256]{1,0:T(8,128)}, u32[]{:S(2)}, u32[]{:S(2)}) %collective-permute-start.6) | collective-permute-done | bytes 524320 | tf_op jit(solution)/shard_map/ppermute | solution.py:20
  85.9 11.9 %collective-permute-done.7 = f32[512,256]{1,0:T(8,128)} collective-permute-done((f32[512,256]{1,0:T(8,128)}, f32[512,256]{1,0:T(8,128)}, u32[]{:S(2)}, u32[]{:S(2)}) %collective-permute-start.7) | collective-permute-done | bytes 524320 | tf_op jit(solution)/shard_map/ppermute | solution.py:21
  97.9 7.6 %fusion.55 = bf16[1,512,256]{2,1,0:T(8,128)(2,1)} fusion(f32[512,256]{1,0:T(8,128)} %fusion.43, f32[512,256]{1,0:T(8,128)} %param.13, f32[512,1536]{0,1:T(8,128)S(1)} %fusion.15, f32[512,256]{1,0:T(8,128)} %collective-permute-done.7, f32[512,256]{1,0:T(8,128)} %collective-permute-done.6, f32[512]{0:T(512)S(1)} %copy-done.5, f32[512]{0:T(512)S(1)} %multiply_add_fusion), kind=kOutput, calls=%fused_computation.41 | convolution fusion | flops 2417491968 | bytes 5509120 | tf_op jit(solution)/shard_map/bij,bjm->bim/dot_general | solution.py:72
  105.5 0.0 all-to-all-done
  105.5 8.5 %while.2 = (s32[]{:T(128)}, f32[4,8,1,2,8,256]{5,4,3,1,2,0:T(8,128)}, bf16[4,8,1,2,8,256]{5,4,3,1,2,0:T(8,128)(2,1)}, bf16[1,512,256]{2,1,0:T(8,128)(2,1)S(1)}, ...) while((s32[]{:T(128)}, ...), condition=%wide.region_7.8_spmd, body=%wide.region_6.7_spmd.sunk | while | flops 67297280 | bytes 855321 | solution.py:115
  105.6 0.1 divide_multiply_fusion.2
  105.7 2.0 %fusion.82 = f32[4,8,1,2,8,256]{5,4,3,1,2,0:T(8,128)} fusion(f32[4,8,1,2,8,256]{5,4,3,1,2,0:T(8,128)} %get-tuple-element.174, s32[]{:T(128)} %get-tuple-element.173, bf16[1,512,256]{2,1,0:T(8,128)(2,1)} %get-tuple-element.187, bf16[1,512,256]{2,1,0:T(8,128)(2,1)S(1)} %get-tuple-element.184, f32[8,2,512]{2,1,0:T(2,128)S(1)} %copy.54, ...), kind=kOutput, calls=%fused_computation.8.clone.1 | convolution fusion | flops 67239936 | bytes 754688 | tf_op jit(solution)/shard_map/while/body/eval_jaxpr/gokrj,ojm->gokrm/dot_general | solution.py:113
  107.7 0.1 divide_multiply_fusion.2
  107.8 2.0 %fusion.82 = f32[4,8,1,2,8,256]{5,4,3,1,2,0:T(8,128)} fusion(f32[4,8,1,2,8,256]{5,4,3,1,2,0:T(8,128)} %get-tuple-element.174, s32[]{:T(128)} %get-tuple-element.173, bf16[1,512,256]{2,1,0:T(8,128)(2,1)} %get-tuple-element.187, bf16[1,512,256]{2,1,0:T(8,128)(2,1)S(1)} %get-tuple-element.184, f32[8,2,512]{2,1,0:T(2,128)S(1)} %copy.54, ...), kind=kOutput, calls=%fused_computation.8.clone.1 | convolution fusion | flops 67239936 | bytes 754688 | tf_op jit(solution)/shard_map/while/body/eval_jaxpr/gokrj,ojm->gokrm/dot_general | solution.py:113
  109.8 0.1 divide_multiply_fusion.2
  109.9 2.0 %fusion.82 = f32[4,8,1,2,8,256]{5,4,3,1,2,0:T(8,128)} fusion(f32[4,8,1,2,8,256]{5,4,3,1,2,0:T(8,128)} %get-tuple-element.174, s32[]{:T(128)} %get-tuple-element.173, bf16[1,512,256]{2,1,0:T(8,128)(2,1)} %get-tuple-element.187, bf16[1,512,256]{2,1,0:T(8,128)(2,1)S(1)} %get-tuple-element.184, f32[8,2,512]{2,1,0:T(2,128)S(1)} %copy.54, ...), kind=kOutput, calls=%fused_computation.8.clone.1 | convolution fusion | flops 67239936 | bytes 754688 | tf_op jit(solution)/shard_map/while/body/eval_jaxpr/gokrj,ojm->gokrm/dot_general | solution.py:113
  111.9 0.1 divide_multiply_fusion.2
  112.0 2.0 %fusion.82 = f32[4,8,1,2,8,256]{5,4,3,1,2,0:T(8,128)} fusion(f32[4,8,1,2,8,256]{5,4,3,1,2,0:T(8,128)} %get-tuple-element.174, s32[]{:T(128)} %get-tuple-element.173, bf16[1,512,256]{2,1,0:T(8,128)(2,1)} %get-tuple-element.187, bf16[1,512,256]{2,1,0:T(8,128)(2,1)S(1)} %get-tuple-element.184, f32[8,2,512]{2,1,0:T(2,128)S(1)} %copy.54, ...), kind=kOutput, calls=%fused_computation.8.clone.1 | convolution fusion | flops 67239936 | bytes 754688 | tf_op jit(solution)/shard_map/while/body/eval_jaxpr/gokrj,ojm->gokrm/dot_general | solution.py:113
  114.1 3.4 %all-to-all-start.2 = ((f32[32,1,2,8,256]{4,3,2,1,0:T(8,128)}), f32[32,1,2,8,256]{4,3,2,1,0:T(8,128)S(1)}, u32[]{:S(2)}, u32[]{:S(2)}) async-start(f32[32,1,2,8,256]{4,3,2,1,0:T(8,128)} %bitcast.107), calls=%async_computation.2 | async-start | bytes 1048576 | tf_op jit(solution)/shard_map/all_to_all | solution.py:123
  117.5 0.1 reshape.298
  117.5 0.9 gather_fusion.2
  118.4 0.1 reshape.301
  118.5 0.1 reshape.266
  118.6 14.2 %all-to-all-done.2 = f32[32,1,2,8,256]{4,3,2,1,0:T(8,128)S(1)} async-done(((f32[32,1,2,8,256]{4,3,2,1,0:T(8,128)}), f32[32,1,2,8,256]{4,3,2,1,0:T(8,128)S(1)}, u32[]{:S(2)}, u32[]{:S(2)}) %all-to-all-start.2) | async-done | bytes 524320 | tf_op jit(solution)/shard_map/all_to_all | solution.py:123
  132.8 0.6 gather_fusion.1
  133.4 0.1 select_reduce_fusion
  133.6 0.6 convert_add_fusion
  (33 shorter events, 0.3 us)
Async XLA Ops:
  0.0 42.9 %collective-permute-start = (bf16[512,256]{1,0:T(8,128)(2,1)}, bf16[512,256]{1,0:T(8,128)(2,1)S(1)}, u32[]{:S(2)}, u32[]{:S(2)}) collective-permute-start(bf16[512,256]{1,0:T(8,128)(2,1)} %param.12), channel_id=1, source_target_pairs={{0,1},{1,2},{2,3},{3,4},{4,5},{5,6},{6,7},{7,8},{8,9},{9,10},{10,1... | collective-permute-start | bytes 786440 | tf_op jit(solution)/shard_map/ppermute | solution.py:20
  4.0 39.6 %collective-permute-start.1 = (bf16[512,256]{1,0:T(8,128)(2,1)}, bf16[512,256]{1,0:T(8,128)(2,1)}, u32[]{:S(2)}, u32[]{:S(2)}) collective-permute-start(bf16[512,256]{1,0:T(8,128)(2,1)} %param.12), channel_id=1, source_target_pairs={{1,0},{2,1},{3,2},{4,3},{5,4},{6,5},{7,6},{8,7},{9,8},{10,9},{11,1... | collective-permute-start | bytes 786440 | tf_op jit(solution)/shard_map/ppermute | solution.py:21
  8.5 29.5 %collective-permute-start.2 = (s32[512]{0:T(512)}, s32[512]{0:T(512)S(1)}, u32[]{:S(2)}, u32[]{:S(2)}) collective-permute-start(s32[512]{0:T(512)} %param.15), channel_id=1, source_target_pairs={{0,1},{1,2},{2,3},{3,4},{4,5},{5,6},{6,7},{7,8},{8,9},{9,10},{10,1... | collective-permute-start | bytes 6152 | tf_op jit(solution)/shard_map/ppermute | solution.py:20
  10.5 31.7 %collective-permute-start.3 = (s32[512]{0:T(512)}, s32[512]{0:T(512)S(1)}, u32[]{:S(2)}, u32[]{:S(2)}) collective-permute-start(s32[512]{0:T(512)} %param.15), channel_id=1, source_target_pairs={{1,0},{2,1},{3,2},{4,3},{5,4},{6,5},{7,6},{8,7},{9,8},{10,9},{11,1... | collective-permute-start | bytes 6152 | tf_op jit(solution)/shard_map/ppermute | solution.py:21
  24.5 54.7 %all-to-all-start.1 = ((s32[32,1,2]{2,1,0:T(1,128)}), s32[32,1,2]{2,1,0:T(1,128)S(1)}, u32[]{:S(2)}, u32[]{:S(2)}) async-start(s32[32,1,2]{2,1,0:T(1,128)} %copy.45), calls=%async_computation.1 | async-start | bytes 32768 | tf_op jit(solution)/shard_map/all_to_all | solution.py:104
  33.1 17.2 %collective-permute-start.4 = (f32[512,256]{1,0:T(8,128)S(1)}, f32[512,256]{1,0:T(8,128)S(1)}, u32[]{:S(2)}, u32[]{:S(2)}) collective-permute-start(f32[512,256]{1,0:T(8,128)S(1)} %broadcast_divide_fusion), channel_id=1, source_target_pairs={{0,1},{1,2},{2,3},{3,4},{4,5},{5,6},{6,7},{7,8},{8,9},{9,10},{10,1... | collective-permute-start | bytes 1572872 | tf_op jit(solution)/shard_map/ppermute | solution.py:20
  38.0 24.4 %collective-permute-start.5 = (f32[512,256]{1,0:T(8,128)S(1)}, f32[512,256]{1,0:T(8,128)S(1)}, u32[]{:S(2)}, u32[]{:S(2)}) collective-permute-start(f32[512,256]{1,0:T(8,128)S(1)} %broadcast_divide_fusion), channel_id=1, source_target_pairs={{1,0},{2,1},{3,2},{4,3},{5,4},{6,5},{7,6},{8,7},{9,8},{10,9},{11,1... | collective-permute-start | bytes 1572872 | tf_op jit(solution)/shard_map/ppermute | solution.py:21
  42.9 19.6 %copy-start.1 = (f32[512,256]{1,0:T(8,128)S(1)}, f32[512,256]{1,0:T(8,128)}, u32[]{:S(2)}) copy-start(f32[512,256]{1,0:T(8,128)} %param.13) | copy-start | bytes 1572868
  42.9 19.6 %copy-start.5 = (f32[512]{0:T(512)S(1)}, f32[512]{0:T(512)}, u32[]{:S(2)}) copy-start(f32[512]{0:T(512)} %param.14) | copy-start | bytes 6148
  42.9 0.7 copy-start.6
  68.5 17.4 %collective-permute-start.6 = (f32[512,256]{1,0:T(8,128)}, f32[512,256]{1,0:T(8,128)}, u32[]{:S(2)}, u32[]{:S(2)}) collective-permute-start(f32[512,256]{1,0:T(8,128)} %fusion.43), channel_id=1, source_target_pairs={{0,1},{1,2},{2,3},{3,4},{4,5},{5,6},{6,7},{7,8},{8,9},{9,10},{10,1... | collective-permute-start | bytes 1572872 | tf_op jit(solution)/shard_map/ppermute | solution.py:20
  70.7 27.2 %collective-permute-start.7 = (f32[512,256]{1,0:T(8,128)}, f32[512,256]{1,0:T(8,128)}, u32[]{:S(2)}, u32[]{:S(2)}) collective-permute-start(f32[512,256]{1,0:T(8,128)} %fusion.43), channel_id=1, source_target_pairs={{1,0},{2,1},{3,2},{4,3},{5,4},{6,5},{7,6},{8,7},{9,8},{10,9},{11,1... | collective-permute-start | bytes 1572872 | tf_op jit(solution)/shard_map/ppermute | solution.py:21
  79.2 26.3 %all-to-all-start = ((bf16[32,1,2,8,256]{4,3,2,1,0:T(8,128)(2,1)}), bf16[32,1,2,8,256]{4,3,2,1,0:T(8,128)(2,1)}, u32[]{:S(2)}, u32[]{:S(2)}) async-start(bf16[32,1,2,8,256]{4,3,2,1,0:T(8,128)(2,1)} %select_multiply_fusion), calls=%async_computation | async-start | bytes 524288 | tf_op jit(solution)/shard_map/all_to_all | solution.py:103
  83.3 22.2 %copy-start = (bf16[512,256]{1,0:T(8,128)(2,1)S(1)}, bf16[512,256]{1,0:T(8,128)(2,1)}, u32[]{:S(2)}) copy-start(bf16[512,256]{1,0:T(8,128)(2,1)} %param.12) | copy-start | bytes 786436
  83.3 22.2 %copy-start.3 = (s32[512]{0:T(512)S(1)}, s32[512]{0:T(512)}, u32[]{:S(2)}) copy-start(s32[512]{0:T(512)} %param.15) | copy-start | bytes 6148
  105.5 11.9 %copy-start.4 = (s32[8,5]{1,0:T(8,128)S(1)}, s32[8,5]{1,0:T(8,128)}, u32[]{:S(2)}) copy-start(s32[8,5]{1,0:T(8,128)} %param.11) | copy-start | bytes 484
  114.1 19.5 %copy-start.2 = (bf16[8,8,256]{2,1,0:T(8,128)(2,1)S(1)}, bf16[8,8,256]{2,1,0:T(8,128)(2,1)}, u32[]{:S(2)}) copy-start(bf16[8,8,256]{2,1,0:T(8,128)(2,1)} %param.9) | copy-start | bytes 98308
  114.1 18.8 %all-to-all-start.2 = ((f32[32,1,2,8,256]{4,3,2,1,0:T(8,128)}), f32[32,1,2,8,256]{4,3,2,1,0:T(8,128)S(1)}, u32[]{:S(2)}, u32[]{:S(2)}) async-start(f32[32,1,2,8,256]{4,3,2,1,0:T(8,128)} %bitcast.107), calls=%async_computation.2 | async-start | bytes 1048576 | tf_op jit(solution)/shard_map/all_to_all | solution.py:123
where the time goes:
time: 135 us; the launch traced here: 134 us
  waiting for transfers between devices  44.8 us (33%)
  starting transfers between devices  43.6 us (32%)
  matrix products  24.3 us (18%)
  other arithmetic  13.4 us (10%)
  local copies, waits for them, and re-layouts  7.61 us (6%)
    ppermute x4, waiting for transfers between devices, with_halo(): after = lax.ppermute(initial, axis, down)  24.1 us
    ppermute x4, starting transfers between devices, with_halo(): after = lax.ppermute(initial, axis, down)  19.2 us
    all_to_all x1, waiting for transfers between devices, shards(): lax.all_to_all(answers, ('atm', 'ocn'), split_axis=0, concat_axis=0, tile...  14.2 us
    dot_general x2, matrix products, shards(): jnp.einsum('bij,bjm->bim', tapered, near_w, precision=lax.Precision.HIGHE...  13.7 us
    ppermute x4, starting transfers between devices, with_halo(): before = lax.ppermute(last, axis, up)  11.4 us
    dot_general x4, matrix products, group_gain(): jnp.einsum('gokrj,ojm->gokrm', gain, weight_rows, preferred_element_type=...  7.97 us
    ppermute x4, waiting for transfers between devices, with_halo(): before = lax.ppermute(last, axis, up)  6.54 us
    all_to_all x1, starting transfers between devices, shards(): lax.all_to_all(places, ('atm', 'ocn'), split_axis=0, concat_axis=0, tiled...  5.55 us
  transfers between devices with their start and end apart: 11, of which 5 were waited for; matrix products, arithmetic and copies ran while one was open for 26% of the time, Pallas kernels for 0%

commit v1 on v0

v1 whole, which is shorter than its diff:
```python
import functools

import jax
import jax.numpy as jnp
import numpy as np
from jax import lax
from jax.experimental import pallas as pl
from jax.experimental.pallas import tpu as pltpu
from jax.sharding import PartitionSpec as P

OBS_BLOCK = 512
READS = 5
CAP = 2
SWEEPS = 2
LENGTH = 16384
LANES = 128
PARTS = OBS_BLOCK // LANES
AXES = ("atm", "ocn")
RELOCATE = True


def homes(atm, ocn):
    places = []
    for column in range(atm // 2):
        chips = range(ocn) if column % 2 == 0 else range(ocn - 1, -1, -1)
        for chip in chips:
            for core in range(2):
                places.append((2 * column + core) * ocn + chip)
    return places


def as_row(ref, start):
    return jnp.concatenate([ref[start + i : start + i + 1, :] for i in range(PARTS)], axis=1)


def as_column(ref, start, part):
    shape = (LANES, LANES)
    diagonal = lax.broadcasted_iota(jnp.int32, shape, 0) == lax.broadcasted_iota(jnp.int32, shape, 1)
    row = jnp.broadcast_to(ref[start + part : start + part + 1, :], shape)
    return jnp.sum(jnp.where(diagonal, row, 0.0), axis=1, keepdims=True)


def split(values):
    high = values.astype(jnp.bfloat16)
    return high, (values - high.astype(jnp.float32)).astype(jnp.bfloat16)


def start_kernel(inverse, y_ref, meta_ref, target_ref, weights_ref):
    for part in range(PARTS):
        rows = pl.ds(part * LANES, LANES)
        y = y_ref[rows, :].astype(jnp.float32)
        divisor = jnp.sum(y * y, axis=1, keepdims=True) * inverse + as_column(meta_ref, PARTS, part)
        weights_ref[rows, :] = target_ref[rows, :] / divisor


def couple_kernel(inverse, ends_ref, y_ref, before_ref, after_ref, meta_ref, meta_before_ref, meta_after_ref, high_ref, low_ref):
    neighbours = ((before_ref, meta_before_ref, ends_ref[0]), (y_ref, meta_ref, 1), (after_ref, meta_after_ref, ends_ref[1]))
    for part in range(PARTS):
        rows = pl.ds(part * LANES, LANES)
        y = y_ref[rows, :]
        wide = y.astype(jnp.float32)
        divisor = jnp.sum(wide * wide, axis=1, keepdims=True) * inverse + as_column(meta_ref, PARTS, part)
        place = as_column(meta_ref, 0, part)
        for number, (other_ref, other_meta_ref, present) in enumerate(neighbours):
            product = lax.dot_general(
                y, other_ref[...], (((1,), (1,)), ((), ())), preferred_element_type=jnp.float32
            )
            spread = (place - as_row(other_meta_ref, 0)) * (1.0 / LENGTH)
            coupling = product * (-inverse / (divisor * (1.0 + spread * spread)))
            if number == 1:
                shape = (LANES, OBS_BLOCK)
                own = lax.broadcasted_iota(jnp.int32, shape, 0) + part * LANES
                coupling = jnp.where(own == lax.broadcasted_iota(jnp.int32, shape, 1), 0.0, coupling)
            else:
                coupling = jnp.where(present > 0, coupling, 0.0)
            high, low = split(coupling)
            columns = pl.ds(number * OBS_BLOCK, OBS_BLOCK)
            high_ref[rows, columns] = high
            low_ref[rows, columns] = low


def coupled(high_ref, low_ref, before_ref, own_ref, after_ref):
    total = None
    for number, ref in enumerate((before_ref, own_ref, after_ref)):
        high, low = split(ref[...])
        columns = pl.ds(number * OBS_BLOCK, OBS_BLOCK)
        for left, right in ((high_ref, high), (low_ref, high), (high_ref, low)):
            term = jnp.dot(left[:, columns], right, preferred_element_type=jnp.float32)
            total = term if total is None else total + term
    return total


def sweep_kernel(high_ref, low_ref, start_ref, before_ref, own_ref, after_ref, weights_ref):
    weights_ref[...] = start_ref[...] + coupled(high_ref, low_ref, before_ref, own_ref, after_ref)


def answer_kernel(high_ref, low_ref, start_ref, before_ref, own_ref, after_ref, gain_ref, answer_ref):
    weights = start_ref[...] + coupled(high_ref, low_ref, before_ref, own_ref, after_ref)
    answer_ref[...] = jnp.dot(
        gain_ref[...], weights.astype(jnp.bfloat16), preferred_element_type=jnp.float32
    )


def gain_kernel(inverse, lines, place_ref, rows_ref, y_ref, meta_ref, gain_ref, product_ref):
    product_ref[...] = lax.dot_general(
        rows_ref[...], y_ref[...], (((1,), (1,)), ((), ())), preferred_element_type=jnp.float32
    )
    height = CAP * lines
    here = jnp.broadcast_to(as_row(meta_ref, 0), (height, OBS_BLOCK))
    slot = lax.broadcasted_iota(jnp.int32, (height, OBS_BLOCK), 0) // lines

    def group(number, carry):
        rows = pl.ds(pl.multiple_of(number * height, height), height)
        place = jnp.full((height, OBS_BLOCK), place_ref[number * CAP], jnp.int32)
        for extra in range(1, CAP):
            place = jnp.where(slot == extra, place_ref[number * CAP + extra], place)
        spread = (place.astype(jnp.float32) - here) * (1.0 / LENGTH)
        gain = product_ref[rows, :] * inverse / (1.0 + spread * spread)
        gain_ref[rows, :] = gain.astype(jnp.bfloat16)
        return carry

    lax.fori_loop(0, gain_ref.shape[0] // height, group, 0, unroll=2)


def request_kernel(home_ref, reads_ref, place_ref, prior_ref, send_ref, send_place_ref, slot_ref, count_ref):
    tiles, lines, members = prior_ref.shape
    slots = send_ref.shape[0]
    send_ref[...] = jnp.zeros_like(send_ref)

    def clear(number, carry):
        for extra in range(CAP):
            send_place_ref[number * CAP + extra] = 0
        count_ref[number] = 0
        return carry

    lax.fori_loop(0, slots // CAP, clear, 0)

    def tile(number, carry):
        states = prior_ref[number].astype(jnp.float32)
        mean = jnp.sum(states, axis=1, keepdims=True) * (1.0 / members)
        anomalies = (states - mean).astype(send_ref.dtype)
        for read in range(READS):
            block = home_ref[reads_ref[number * READS + read]]
            used = count_ref[block]
            count_ref[block] = used + 1
            slot = block * CAP + jnp.minimum(used, CAP - 1)
            send_ref[slot] = anomalies
            send_place_ref[slot] = place_ref[number]
            slot_ref[number * READS + read] = slot
        return carry

    lax.fori_loop(0, tiles, tile, 0)


def collect_kernel(slot_ref, prior_ref, returned_ref, out_ref):
    def tile(number, carry):
        total = returned_ref[slot_ref[number * READS]]
        for read in range(1, READS):
            total = total + returned_ref[slot_ref[number * READS + read]]
        out_ref[number] = prior_ref[number].astype(jnp.float32) + total
        return carry

    lax.fori_loop(0, prior_ref.shape[0], tile, 0)


VMEM = pl.BlockSpec(memory_space=pltpu.VMEM)
SMEM = pl.BlockSpec(memory_space=pltpu.SMEM)


def call(kernel, ins, outs, name, scratch=()):
    shapes = [jax.ShapeDtypeStruct(shape, dtype) for shape, dtype, _ in outs]
    specs = [space for _, _, space in outs]
    single = len(outs) == 1
    return pl.pallas_call(
        kernel,
        in_specs=list(ins),
        out_shape=shapes[0] if single else shapes,
        out_specs=specs[0] if single else specs,
        scratch_shapes=list(scratch),
        name=name,
    )


def shards(
    home,
    prior_states,
    patch_mesh_location,
    fetched_blocks,
    measured_deviations,
    departure_vectors,
    measurement_error_spread,
    measurement_mesh_location,
):
    f32, bf16, i32 = jnp.float32, jnp.bfloat16, jnp.int32
    tiles, lines, members = prior_states.shape
    inverse = 1.0 / (members - 1)
    devices = len(home)
    slots = devices * CAP
    rows = slots * lines
    up = [(home[k], home[(k + 1) % devices]) for k in range(devices)]
    down = [(b, a) for a, b in up]
    move = [(k, home[k]) for k in range(devices)]
    block_of = np.argsort(np.array(home))
    relocated = home != list(range(devices))

    def send(values, pairs):
        return lax.ppermute(values, AXES, pairs)

    def relocate(values):
        return send(values, move) if relocated else values

    square = (OBS_BLOCK, members)
    meta = jnp.concatenate(
        [measurement_mesh_location.astype(f32), measurement_error_spread]
    ).reshape(2 * PARTS, LANES)
    y = relocate(measured_deviations)
    start = call(
        functools.partial(start_kernel, inverse), [VMEM] * 3, [(square, f32, VMEM)], "start"
    )(measured_deviations, meta, departure_vectors)
    meta = relocate(meta)
    start = relocate(start)

    y_before, y_after = send(y, up), send(y, down)
    meta_before, meta_after = send(meta, up), send(meta, down)
    w_before, w_after = send(start, up), send(start, down)

    send_rows, send_places, slot = call(
        request_kernel,
        [SMEM, SMEM, SMEM, VMEM],
        [((slots, lines, members), bf16, VMEM), ((slots,), i32, SMEM), ((tiles * READS,), i32, SMEM)],
        "request",
        [pltpu.SMEM((devices,), i32)],
    )(jnp.asarray(home, i32), fetched_blocks.reshape(-1), patch_mesh_location, prior_states)
    places = lax.all_to_all(send_places.reshape(devices, 1, CAP), AXES, 0, 0, tiled=True)
    arrived = lax.all_to_all(
        send_rows.reshape(devices, CAP, lines, members), AXES, 0, 0, tiled=True
    )

    me = lax.axis_index(AXES)
    here = jnp.asarray(block_of, i32)[me]
    ends = jnp.stack([here, devices - 1 - here])
    wide = (OBS_BLOCK, 3 * OBS_BLOCK)
    high, low = call(
        functools.partial(couple_kernel, inverse),
        [SMEM] + [VMEM] * 6,
        [(wide, bf16, VMEM), (wide, bf16, VMEM)],
        "couple",
    )(ends, y, y_before, y_after, meta, meta_before, meta_after)
    gain = call(
        functools.partial(gain_kernel, inverse, lines),
        [SMEM] + [VMEM] * 3,
        [((rows, OBS_BLOCK), bf16, VMEM)],
        "gain",
        [pltpu.VMEM((rows, OBS_BLOCK), f32)],
    )(places.reshape(-1), arrived.reshape(rows, members), y, meta)

    weights = call(sweep_kernel, [VMEM] * 6, [(square, f32, VMEM)], "sweep")(
        high, low, start, w_before, start, w_after
    )
    w_before, w_after = send(weights, up), send(weights, down)
    answers = call(answer_kernel, [VMEM] * 7, [((rows, members), f32, VMEM)], "answer")(
        high, low, start, w_before, weights, w_after, gain
    )
    returned = lax.all_to_all(
        answers.reshape(devices, CAP, lines, members), AXES, 0, 0, tiled=True
    )
    return call(collect_kernel, [SMEM, VMEM, VMEM], [((tiles, lines, members), f32, VMEM)], "collect")(
        slot, prior_states, returned.reshape(slots, lines, members)
    )


def solution(mesh):
    atm, ocn = mesh.shape["atm"], mesh.shape["ocn"]
    home = homes(atm, ocn) if RELOCATE else list(range(atm * ocn))
    placed = (
        P(AXES, None, None),
        P(AXES),
        P(AXES, None),
        P(AXES, None),
        P(AXES, None),
        P(AXES),
        P(AXES),
    )
    return jax.shard_map(
        functools.partial(shards, home),
        mesh=mesh,
        in_specs=placed,
        out_specs=P(AXES, None, None),
        check_vma=False,
    )
```

time: 135 us -> 115 us (0.85)
  blocking collectives: 0 us -> 28.2 us
  waiting for transfers between devices: 44.8 us -> 20 us
  matrix products: 24.3 us -> 0 us
  Pallas kernels: 0 us -> 23.4 us
  starting transfers between devices: 43.6 us -> 29.9 us
  other arithmetic: 13.4 us -> 3.83 us
    all_to_all x0 -> x2, blocking collectives: none -> 28.2 us  [the longest x1 18.5 us: shards(): lax.all_to_all(answers.reshape(devices, CAP, lines, members), AXES, 0, 0,...]
    dot_general x7 -> x0, matrix products: 24.3 us -> none  [the longest x2 13.7 us: shards(): jnp.einsum('bij,bjm->bim', tapered, near_w, precision=lax.Precision.HIGHE...]
    pallas_call x0 -> x7, Pallas kernels: none -> 23.4 us  [the longest x1 5.26 us: shards(): call(answer_kernel, [VMEM] * 7, [((rows, members), f32, VMEM)], 'answer')]
    ppermute x8 -> x11, waiting for transfers between devices: 30.6 us -> 11.3 us  [send(): return lax.ppermute(values, AXES, pairs)]
    all_to_all x3 -> x1, starting transfers between devices: 13 us -> 2.93 us  [shards(): lax.all_to_all(send_rows.reshape(devices, CAP, lines, members), AXES, 0,...]
    all_to_all x3 -> x1, waiting for transfers between devices: 14.2 us -> 8.75 us  [shards(): lax.all_to_all(send_rows.reshape(devices, CAP, lines, members), AXES, 0,...]
    gather x4 -> x0, other arithmetic: 4.99 us -> none  [the longest x1 4.96 us: shards(): jnp.take(patch_mesh_location, source) * filled]
    gather x8 -> x0, local copies, waits for them, and re-layouts: 4.72 us -> none  [the longest x3 1.81 us: shards(): jnp.take(patch_mesh_location, source) * filled]
  transfers between devices with their start and end apart: 11 -> 12, of which waited for: 5 -> 5; matrix products, arithmetic and copies ran while one was open for 26% -> 5% of each run, Pallas kernels for 0% -> 8%
where the time goes in v1:
time: 115 us; the launch traced here: 114 us
  starting transfers between devices  29.9 us (26%)
  blocking collectives  28.2 us (25%)
  Pallas kernels  23.4 us (20%)
  waiting for transfers between devices  20 us (17%)
  local copies, waits for them, and re-layouts  8.34 us (7%)
  other arithmetic  3.83 us (3%)
    ppermute x11, starting transfers between devices, send(): return lax.ppermute(values, AXES, pairs)  27 us
    all_to_all x1, blocking collectives, shards(): lax.all_to_all(answers.reshape(devices, CAP, lines, members), AXES, 0, 0,...  18.5 us
    ppermute x11, waiting for transfers between devices, send(): return lax.ppermute(values, AXES, pairs)  11.3 us
    all_to_all x1, blocking collectives, shards(): lax.all_to_all(send_places.reshape(devices, 1, CAP), AXES, 0, 0, tiled=True)  9.75 us
    all_to_all x1, waiting for transfers between devices, shards(): lax.all_to_all(send_rows.reshape(devices, CAP, lines, members), AXES, 0,...  8.75 us
    pallas_call x1, Pallas kernels, shards(): call(answer_kernel, [VMEM] * 7, [((rows, members), f32, VMEM)], 'answer')  5.26 us
    pallas_call x1, Pallas kernels, shards(): call(sweep_kernel, [VMEM] * 6, [(square, f32, VMEM)], 'sweep')  4.64 us
    unnamed x26, local copies, waits for them, and re-layouts  4.62 us
  transfers between devices with their start and end apart: 12, of which 5 were waited for; matrix products, arithmetic and copies ran while one was open for 5% of the time, Pallas kernels for 8%

profile of v1, /device:TPU:1, one launch (start us, length us, event | category | flops | bytes accessed | tf_op | source)
XLA Modules:
  0.0 114.5 jit_solution(15052255468848965443)
XLA Ops:
  0.0 0.7 convert_bitcast_fusion
  0.7 1.3 %pad_maximum_fusion.meta_ref = f32[8,128]{1,0:T(8,128)} fusion(f32[4,128]{1,0:T(4,128)} %bitcast.13, f32[4,128]{1,0:T(4,128)S(1)} %convert_bitcast_fusion), kind=kLoop, calls=%fused_computation | loop fusion | flops 1024 | bytes 8192 | tf_op jit(solution)/shard_map/concatenate | solution.py:213
  2.0 2.2 %start.1 = f32[512,256]{1,0:T(8,128)} custom-call(bf16[512,256]{1,0:T(8,128)(2,1)} %y_ref.1, f32[8,128]{1,0:T(8,128)} %pad_maximum_fusion.meta_ref, f32[512,256]{1,0:T(8,128)} %target_ref.1), custom_call_target="tpu_custom_call" | custom-call | tf_op jit(solution)/shard_map/start/pallas_call | solution.py:217
  4.1 5.6 %collective-permute-start.6 = (f32[512,256]{1,0:T(8,128)}, f32[512,256]{1,0:T(8,128)S(1)}, u32[]{:S(2)}, u32[]{:S(2)}) collective-permute-start(f32[512,256]{1,0:T(8,128)} %start.1), channel_id=1, source_target_pairs={{0,0},{1,4},{2,1},{3,5},{4,2},{5,6},{6,3},{7,7},{8,11},{9,15},{10,... | collective-permute-start | bytes 1572872 | tf_op jit(solution)/shard_map/ppermute | solution.py:207
  9.7 2.4 %collective-permute-start = (bf16[512,256]{1,0:T(8,128)(2,1)}, bf16[512,256]{1,0:T(8,128)(2,1)S(1)}, u32[]{:S(2)}, u32[]{:S(2)}) collective-permute-start(bf16[512,256]{1,0:T(8,128)(2,1)} %y_ref.1), channel_id=1, source_target_pairs={{0,0},{1,4},{2,1},{3,5},{4,2},{5,6},{6,3},{7,7},{8,11},{9,15},{10,... | collective-permute-start | bytes 786440 | tf_op jit(solution)/shard_map/ppermute | solution.py:207
  12.1 4.1 %collective-permute-done.6.start_ref.own_ref = f32[512,256]{1,0:T(8,128)S(1)} collective-permute-done((f32[512,256]{1,0:T(8,128)}, f32[512,256]{1,0:T(8,128)S(1)}, u32[]{:S(2)}, u32[]{:S(2)}) %collective-permute-start.6) | collective-permute-done | bytes 524320 | tf_op jit(solution)/shard_map/ppermute | solution.py:207
  16.2 0.0 copy-start
  16.2 0.0 collective-permute-start.8
  16.2 10.3 %collective-permute-start.7 = (f32[512,256]{1,0:T(8,128)S(1)}, f32[512,256]{1,0:T(8,128)S(1)}, u32[]{:S(2)}, u32[]{:S(2)}) collective-permute-start(f32[512,256]{1,0:T(8,128)S(1)} %collective-permute-done.6.start_ref.own_ref), channel_id=1, source_target_pairs={{0,4},{4,1},{1,5},{5,2},{2,6},{6,3},{3,7},{7,11},{11,15},{15,10},{... | collective-permute-start | bytes 1572872 | tf_op jit(solution)/shard_map/ppermute | solution.py:207
  26.5 0.0 collective-permute-done.y_ref
  26.5 0.0 copy-start.2
  26.5 0.0 collective-permute-start.2
  26.5 2.8 %collective-permute-start.1 = (bf16[512,256]{1,0:T(8,128)(2,1)S(1)}, bf16[512,256]{1,0:T(8,128)(2,1)S(1)}, u32[]{:S(2)}, u32[]{:S(2)}) collective-permute-start(bf16[512,256]{1,0:T(8,128)(2,1)S(1)} %collective-permute-done.y_ref), channel_id=1, source_target_pairs={{0,4},{4,1},{1,5},{5,2},{2,6},{6,3},{3,7},{7,11},{11,15},{15,10},{... | collective-permute-start | bytes 786440 | tf_op jit(solution)/shard_map/ppermute | solution.py:207
  29.3 1.9 %collective-permute-start.3 = (f32[8,128]{1,0:T(8,128)}, f32[8,128]{1,0:T(8,128)S(1)}, u32[]{:S(2)}, u32[]{:S(2)}) collective-permute-start(f32[8,128]{1,0:T(8,128)} %pad_maximum_fusion.meta_ref), channel_id=1, source_target_pairs={{0,0},{1,4},{2,1},{3,5},{4,2},{5,6},{6,3},{7,7},{8,11},{9,15},{10,... | collective-permute-start | bytes 12296 | tf_op jit(solution)/shard_map/ppermute | solution.py:207
  31.2 5.1 %collective-permute-done.3.meta_ref = f32[8,128]{1,0:T(8,128)S(1)} collective-permute-done((f32[8,128]{1,0:T(8,128)}, f32[8,128]{1,0:T(8,128)S(1)}, u32[]{:S(2)}, u32[]{:S(2)}) %collective-permute-start.3) | collective-permute-done | bytes 4128 | tf_op jit(solution)/shard_map/ppermute | solution.py:207
  36.3 0.0 collective-permute-start.5
  36.3 1.3 %dynamic_slice.3 = s32[1]{0:T(128)} dynamic-slice(s32[32]{0:T(128)} %constant.23.clone, s32[]{:T(128)S(6)} %select_n.3), dynamic_slice_sizes={1} | dynamic-slice | bytes 12 | tf_op jit(solution)/shard_map/dynamic_slice | solution.py:240
  38.2 1.1 collective-permute-done.5.meta_after_ref
  39.3 0.0 copy-start.10
  39.3 0.7 collective-permute-start.4
  40.0 1.3 %pad_add_fusion.ends_ref = s32[2]{0:T(128)} fusion(s32[1]{0:T(128)S(6)} %sub.4, s32[1]{0:T(128)} %dynamic_slice.3), kind=kLoop, calls=%fused_computation.2 | loop fusion | flops 2 | bytes 16 | tf_op jit(solution)/shard_map/stack | solution.py:241
  41.3 1.0 collective-permute-done.4.meta_before_ref
  42.3 0.0 copy-start.11
  42.3 0.0 collective-permute-done.2.after_ref
  42.3 0.0 copy-start.7
  42.3 0.0 collective-permute-done.1.before_ref
  42.3 0.0 copy-done.2
  42.3 0.0 copy-done.9
  42.4 0.0 copy-done.10
  42.4 0.5 copy-done.11
  42.9 0.1 copy-done.7
  43.0 0.0 copy-start.8
  43.0 0.7 copy-done.8
  43.7 4.5 %couple.1 = (bf16[512,1536]{1,0:T(8,128)(2,1)}, bf16[512,1536]{1,0:T(8,128)(2,1)}) custom-call(s32[2]{0:T(128)} %pad_add_fusion.ends_ref, bf16[512,256]{1,0:T(8,128)(2,1)} %copy-done.2, bf16[512,256]{1,0:T(8,128)(2,1)} %copy-done.8, bf16[512,256]{1,0:T(8,128)(2,1)} %copy-done.7, f32[8,128]{1,0:T(8,128)} %copy-done.9, f32[8,128]{1,0:T(8,128)} %copy-done.11, ...), custom_call_target="tpu_custom_call" | custom-call | tf_op jit(solution)/shard_map/couple/pallas_call | solution.py:243
  48.2 0.0 collective-permute-done.8.after_ref
  48.2 0.0 copy-start.5
  48.2 0.0 collective-permute-done.7.before_ref
  48.2 0.0 copy-start.6
  48.2 0.0 copy-done
  48.2 0.8 copy-done.5
  49.0 0.2 copy-done.6
  49.2 0.0 copy-start.12
  49.2 4.6 %sweep.1.own_ref = f32[512,256]{1,0:T(8,128)} custom-call(bf16[512,1536]{1,0:T(8,128)(2,1)} %get-tuple-element.11.high_ref, bf16[512,1536]{1,0:T(8,128)(2,1)} %get-tuple-element.12.low_ref, f32[512,256]{1,0:T(8,128)} %copy-done, f32[512,256]{1,0:T(8,128)} %copy-done.6, f32[512,256]{1,0:T(8,128)} %copy-done, f32[512,256]{1,0:T(8,128)} %copy-done.5), custom_call_target="tpu_custom_call" | custom-call | tf_op jit(solution)/shard_map/sweep/pallas_call | solution.py:257
  53.8 3.3 %collective-permute-start.10 = (f32[512,256]{1,0:T(8,128)}, f32[512,256]{1,0:T(8,128)S(1)}, u32[]{:S(2)}, u32[]{:S(2)}) collective-permute-start(f32[512,256]{1,0:T(8,128)} %sweep.1.own_ref), channel_id=1, source_target_pairs={{4,0},{1,4},{5,1},{2,5},{6,2},{3,6},{7,3},{11,7},{15,11},{10,15},{... | collective-permute-start | bytes 1572872 | tf_op jit(solution)/shard_map/ppermute | solution.py:207
  57.1 0.0 collective-permute-start.9
  57.1 0.0 copy-done.12
  57.1 0.6 reshape.27.reads_ref
  57.7 2.4 %request.1 = (bf16[64,8,256]{2,1,0:T(8,128)(2,1)}, s32[64]{0:T(128)}, s32[40]{0:T(128)}) custom-call(s32[32]{0:T(128)} %constant.22.clone.home_ref, s32[40]{0:T(128)} %reshape.27.reads_ref, s32[8]{0:T(128)} %place_ref.1, bf16[8,8,256]{2,1,0:T(8,128)(2,1)} %prior_ref.3), custom_call_target="tpu_custom_call" | custom-call | tf_op jit(solution)/shard_map/request/pallas_call | solution.py:227
  60.1 0.8 reshape.28
  60.8 9.8 %all_to_all.15 = s32[32,1,2]{2,1,0:T(1,128)S(1)} all-to-all(s32[32,1,2]{2,1,0:T(1,128)S(1)} %bitcast.12), channel_id=1, replica_groups=mesh['atm'=8,'ocn'=4] {'atm','ocn'}, dimensions={0} | all-to-all | bytes 512 | tf_op jit(solution)/shard_map/all_to_all | solution.py:234
  70.6 2.9 %all-to-all-start.1 = ((bf16[32,2,8,256]{3,2,1,0:T(8,128)(2,1)}), bf16[32,2,8,256]{3,2,1,0:T(8,128)(2,1)S(1)}, u32[]{:S(2)}, u32[]{:S(2)}) async-start(bf16[32,2,8,256]{3,2,1,0:T(8,128)(2,1)} %bitcast.11), calls=%async_computation.1 | async-start | bytes 524288 | tf_op jit(solution)/shard_map/all_to_all | solution.py:235
  73.5 0.5 broadcast.3
  74.0 0.6 reduce.3
  74.6 0.6 reshape.29.place_ref
  75.2 8.8 %all-to-all-done.1 = bf16[32,2,8,256]{3,2,1,0:T(8,128)(2,1)S(1)} async-done(((bf16[32,2,8,256]{3,2,1,0:T(8,128)(2,1)}), bf16[32,2,8,256]{3,2,1,0:T(8,128)(2,1)S(1)}, u32[]{:S(2)}, u32[]{:S(2)}) %all-to-all-start.1) | async-done | bytes 262176 | tf_op jit(solution)/shard_map/all_to_all | solution.py:235
  84.0 0.7 copy-done.1
  84.7 2.6 %gain.1.gain_ref = bf16[512,512]{1,0:T(8,128)(2,1)} custom-call(s32[64]{0:T(128)} %reshape.29.place_ref, bf16[512,256]{1,0:T(8,128)(2,1)} %bitcast.10, bf16[512,256]{1,0:T(8,128)(2,1)} %copy-done.2, f32[8,128]{1,0:T(8,128)} %copy-done.9), custom_call_target="tpu_custom_call" | custom-call | tf_op jit(solution)/shard_map/gain/pallas_call | solution.py:249
  87.3 0.0 collective-permute-done.10.after_ref
  87.3 0.0 collective-permute-done.9.before_ref
  87.3 0.8 copy-done.3
  88.1 0.8 copy-done.4
  88.9 5.3 %answer.1 = f32[512,256]{1,0:T(8,128)} custom-call(bf16[512,1536]{1,0:T(8,128)(2,1)} %get-tuple-element.11.high_ref, bf16[512,1536]{1,0:T(8,128)(2,1)} %get-tuple-element.12.low_ref, f32[512,256]{1,0:T(8,128)} %copy-done, f32[512,256]{1,0:T(8,128)} %copy-done.4, f32[512,256]{1,0:T(8,128)} %sweep.1.own_ref, f32[512,256]{1,0:T(8,128)} %copy-done.3, ...), custom_call_target="tpu_custom_call" | custom-call | tf_op jit(solution)/shard_map/answer/pallas_call | solution.py:261
  94.2 18.5 %all_to_all.16 = f32[32,2,8,256]{3,2,1,0:T(8,128)} all-to-all(f32[32,2,8,256]{3,2,1,0:T(8,128)} %bitcast.8), channel_id=1, replica_groups=mesh['atm'=8,'ocn'=4] {'atm','ocn'}, dimensions={0} | all-to-all | bytes 1048576 | tf_op jit(solution)/shard_map/all_to_all | solution.py:264
  112.7 1.8 %collect.1 = f32[8,8,256]{2,1,0:T(8,128)} custom-call(s32[40]{0:T(128)} %get-tuple-element.10.slot_ref, bf16[8,8,256]{2,1,0:T(8,128)(2,1)} %prior_ref.3, f32[64,8,256]{2,1,0:T(8,128)} %bitcast.9), custom_call_target="tpu_custom_call" | custom-call | tf_op jit(solution)/shard_map/collect/pallas_call | solution.py:267
  (4 shorter events, 0.0 us)
Async XLA Ops:
  4.1 12.1 %collective-permute-start.6 = (f32[512,256]{1,0:T(8,128)}, f32[512,256]{1,0:T(8,128)S(1)}, u32[]{:S(2)}, u32[]{:S(2)}) collective-permute-start(f32[512,256]{1,0:T(8,128)} %start.1), channel_id=1, source_target_pairs={{0,0},{1,4},{2,1},{3,5},{4,2},{5,6},{6,3},{7,7},{8,11},{9,15},{10,... | collective-permute-start | bytes 1572872 | tf_op jit(solution)/shard_map/ppermute | solution.py:207
  9.7 16.8 %collective-permute-start = (bf16[512,256]{1,0:T(8,128)(2,1)}, bf16[512,256]{1,0:T(8,128)(2,1)S(1)}, u32[]{:S(2)}, u32[]{:S(2)}) collective-permute-start(bf16[512,256]{1,0:T(8,128)(2,1)} %y_ref.1), channel_id=1, source_target_pairs={{0,0},{1,4},{2,1},{3,5},{4,2},{5,6},{6,3},{7,7},{8,11},{9,15},{10,... | collective-permute-start | bytes 786440 | tf_op jit(solution)/shard_map/ppermute | solution.py:207
  16.2 32.0 %copy-start = (f32[512,256]{1,0:T(8,128)}, f32[512,256]{1,0:T(8,128)S(1)}, u32[]{:S(2)}) copy-start(f32[512,256]{1,0:T(8,128)S(1)} %collective-permute-done.6.start_ref.own_ref) | copy-start | bytes 1572868
  16.2 32.0 %collective-permute-start.8 = (f32[512,256]{1,0:T(8,128)S(1)}, f32[512,256]{1,0:T(8,128)S(1)}, u32[]{:S(2)}, u32[]{:S(2)}) collective-permute-start(f32[512,256]{1,0:T(8,128)S(1)} %collective-permute-done.6.start_ref.own_ref), channel_id=1, source_target_pairs={{4,0},{1,4},{5,1},{2,5},{6,2},{3,6},{7,3},{11,7},{15,11},{10,15},{... | collective-permute-start | bytes 1572872 | tf_op jit(solution)/shard_map/ppermute | solution.py:207
  16.2 32.0 %collective-permute-start.7 = (f32[512,256]{1,0:T(8,128)S(1)}, f32[512,256]{1,0:T(8,128)S(1)}, u32[]{:S(2)}, u32[]{:S(2)}) collective-permute-start(f32[512,256]{1,0:T(8,128)S(1)} %collective-permute-done.6.start_ref.own_ref), channel_id=1, source_target_pairs={{0,4},{4,1},{1,5},{5,2},{2,6},{6,3},{3,7},{7,11},{11,15},{15,10},{... | collective-permute-start | bytes 1572872 | tf_op jit(solution)/shard_map/ppermute | solution.py:207
  26.5 15.8 %copy-start.2 = (bf16[512,256]{1,0:T(8,128)(2,1)}, bf16[512,256]{1,0:T(8,128)(2,1)S(1)}, u32[]{:S(2)}) copy-start(bf16[512,256]{1,0:T(8,128)(2,1)S(1)} %collective-permute-done.y_ref) | copy-start | bytes 786436
  26.5 15.8 %collective-permute-start.2 = (bf16[512,256]{1,0:T(8,128)(2,1)S(1)}, bf16[512,256]{1,0:T(8,128)(2,1)S(1)}, u32[]{:S(2)}, u32[]{:S(2)}) collective-permute-start(bf16[512,256]{1,0:T(8,128)(2,1)S(1)} %collective-permute-done.y_ref), channel_id=1, source_target_pairs={{4,0},{1,4},{5,1},{2,5},{6,2},{3,6},{7,3},{11,7},{15,11},{10,15},{... | collective-permute-start | bytes 786440 | tf_op jit(solution)/shard_map/ppermute | solution.py:207
  26.5 15.8 %collective-permute-start.1 = (bf16[512,256]{1,0:T(8,128)(2,1)S(1)}, bf16[512,256]{1,0:T(8,128)(2,1)S(1)}, u32[]{:S(2)}, u32[]{:S(2)}) collective-permute-start(bf16[512,256]{1,0:T(8,128)(2,1)S(1)} %collective-permute-done.y_ref), channel_id=1, source_target_pairs={{0,4},{4,1},{1,5},{5,2},{2,6},{6,3},{3,7},{7,11},{11,15},{15,10},{... | collective-permute-start | bytes 786440 | tf_op jit(solution)/shard_map/ppermute | solution.py:207
  29.3 7.0 %collective-permute-start.3 = (f32[8,128]{1,0:T(8,128)}, f32[8,128]{1,0:T(8,128)S(1)}, u32[]{:S(2)}, u32[]{:S(2)}) collective-permute-start(f32[8,128]{1,0:T(8,128)} %pad_maximum_fusion.meta_ref), channel_id=1, source_target_pairs={{0,0},{1,4},{2,1},{3,5},{4,2},{5,6},{6,3},{7,7},{8,11},{9,15},{10,... | collective-permute-start | bytes 12296 | tf_op jit(solution)/shard_map/ppermute | solution.py:207
  36.3 6.1 %copy-start.9 = (f32[8,128]{1,0:T(8,128)}, f32[8,128]{1,0:T(8,128)S(1)}, u32[]{:S(2)}) copy-start(f32[8,128]{1,0:T(8,128)S(1)} %collective-permute-done.3.meta_ref) | copy-start | bytes 12292
  36.3 3.0 %collective-permute-start.5 = (f32[8,128]{1,0:T(8,128)S(1)}, f32[8,128]{1,0:T(8,128)S(1)}, u32[]{:S(2)}, u32[]{:S(2)}) collective-permute-start(f32[8,128]{1,0:T(8,128)S(1)} %collective-permute-done.3.meta_ref), channel_id=1, source_target_pairs={{4,0},{1,4},{5,1},{2,5},{6,2},{3,6},{7,3},{11,7},{15,11},{10,15},{... | collective-permute-start | bytes 12296 | tf_op jit(solution)/shard_map/ppermute | solution.py:207
  39.3 3.0 %copy-start.10 = (f32[8,128]{1,0:T(8,128)}, f32[8,128]{1,0:T(8,128)S(1)}, u32[]{:S(2)}) copy-start(f32[8,128]{1,0:T(8,128)S(1)} %collective-permute-done.5.meta_after_ref) | copy-start | bytes 12292
  39.3 3.0 %collective-permute-start.4 = (f32[8,128]{1,0:T(8,128)S(1)}, f32[8,128]{1,0:T(8,128)S(1)}, u32[]{:S(2)}, u32[]{:S(2)}) collective-permute-start(f32[8,128]{1,0:T(8,128)S(1)} %collective-permute-done.3.meta_ref), channel_id=1, source_target_pairs={{0,4},{4,1},{1,5},{5,2},{2,6},{6,3},{3,7},{7,11},{11,15},{15,10},{... | collective-permute-start | bytes 12296 | tf_op jit(solution)/shard_map/ppermute | solution.py:207
  42.3 0.6 copy-start.11
  42.3 0.7 copy-start.7
  43.0 0.7 copy-start.8
  48.2 0.8 copy-start.5
  48.2 1.0 copy-start.6
  49.2 7.9 %copy-start.12 = (s32[8,5]{1,0:T(8,128)S(1)}, s32[8,5]{1,0:T(8,128)}, u32[]{:S(2)}) copy-start(s32[8,5]{1,0:T(8,128)} %param.11) | copy-start | bytes 484
  53.8 33.5 %collective-permute-start.10 = (f32[512,256]{1,0:T(8,128)}, f32[512,256]{1,0:T(8,128)S(1)}, u32[]{:S(2)}, u32[]{:S(2)}) collective-permute-start(f32[512,256]{1,0:T(8,128)} %sweep.1.own_ref), channel_id=1, source_target_pairs={{4,0},{1,4},{5,1},{2,5},{6,2},{3,6},{7,3},{11,7},{15,11},{10,15},{... | collective-permute-start | bytes 1572872 | tf_op jit(solution)/shard_map/ppermute | solution.py:207
  57.1 30.2 %collective-permute-start.9 = (f32[512,256]{1,0:T(8,128)}, f32[512,256]{1,0:T(8,128)S(1)}, u32[]{:S(2)}, u32[]{:S(2)}) collective-permute-start(f32[512,256]{1,0:T(8,128)} %sweep.1.own_ref), channel_id=1, source_target_pairs={{0,4},{4,1},{1,5},{5,2},{2,6},{6,3},{3,7},{7,11},{11,15},{15,10},{... | collective-permute-start | bytes 1572872 | tf_op jit(solution)/shard_map/ppermute | solution.py:207
  70.6 13.4 %all-to-all-start.1 = ((bf16[32,2,8,256]{3,2,1,0:T(8,128)(2,1)}), bf16[32,2,8,256]{3,2,1,0:T(8,128)(2,1)S(1)}, u32[]{:S(2)}, u32[]{:S(2)}) async-start(bf16[32,2,8,256]{3,2,1,0:T(8,128)(2,1)} %bitcast.11), calls=%async_computation.1 | async-start | bytes 524288 | tf_op jit(solution)/shard_map/all_to_all | solution.py:235
  84.0 0.7 copy-start.1
  87.3 0.8 copy-start.3
  88.1 0.8 copy-start.4

commit v2 on v1

v2 whole, which is shorter than its diff:
```python
import functools

import jax
import jax.numpy as jnp
from jax import lax
from jax.experimental import pallas as pl
from jax.experimental.pallas import tpu as pltpu
from jax.sharding import PartitionSpec as P


OBS_BLOCK = 512
READS = 5
CAP = 2
LENGTH = 16384
LANES = 128
PARTS = OBS_BLOCK // LANES
AXES = ("atm", "ocn")
RELOCATE = True


def homes(atm, ocn):
    places = []
    for column in range(atm // 2):
        chips = range(ocn) if column % 2 == 0 else range(ocn - 1, -1, -1)
        for chip in chips:
            for core in range(2):
                places.append((2 * column + core) * ocn + chip)
    return places


def as_row(ref, start):
    return jnp.concatenate([ref[start + i : start + i + 1, :] for i in range(PARTS)], axis=1)


def as_column(ref, start, part):
    shape = (LANES, LANES)
    diagonal = lax.broadcasted_iota(jnp.int32, shape, 0) == lax.broadcasted_iota(jnp.int32, shape, 1)
    row = jnp.broadcast_to(ref[start + part : start + part + 1, :], shape)
    return jnp.sum(jnp.where(diagonal, row, 0.0), axis=1, keepdims=True)


def split(values):
    high = values.astype(jnp.bfloat16)
    return high, (values - high.astype(jnp.float32)).astype(jnp.bfloat16)


def start_kernel(inverse, y_ref, place_ref, error_ref, target_ref, weights_ref, meta_ref):
    meta_ref[:PARTS, :] = place_ref[...].astype(jnp.float32)
    meta_ref[PARTS:, :] = error_ref[...]
    for part in range(PARTS):
        rows = pl.ds(part * LANES, LANES)
        y = y_ref[rows, :].astype(jnp.float32)
        divisor = jnp.sum(y * y, axis=1, keepdims=True) * inverse + as_column(error_ref, 0, part)
        weights_ref[rows, :] = target_ref[rows, :] / divisor


def couple_kernel(
    inverse, first, last, me_ref, y_ref, before_ref, after_ref, meta_ref, meta_before_ref, meta_after_ref,
    own_high_ref, own_low_ref, near_high_ref, near_low_ref,
):
    near = ((before_ref, meta_before_ref, first), (after_ref, meta_after_ref, last))
    for part in range(PARTS):
        rows = pl.ds(part * LANES, LANES)
        y = y_ref[rows, :]
        wide = y.astype(jnp.float32)
        divisor = jnp.sum(wide * wide, axis=1, keepdims=True) * inverse + as_column(meta_ref, PARTS, part)
        place = as_column(meta_ref, 0, part)

        def coupling(other_ref, other_meta_ref):
            product = lax.dot_general(
                y, other_ref[...], (((1,), (1,)), ((), ())), preferred_element_type=jnp.float32
            )
            spread = (place - as_row(other_meta_ref, 0)) * (1.0 / LENGTH)
            return product * (-inverse / (divisor * (1.0 + spread * spread)))

        shape = (LANES, OBS_BLOCK)
        line = lax.broadcasted_iota(jnp.int32, shape, 0) + part * LANES
        own = jnp.where(line == lax.broadcasted_iota(jnp.int32, shape, 1), 0.0, coupling(y_ref, meta_ref))
        own_high_ref[rows, :], own_low_ref[rows, :] = split(own)
        for number, (other_ref, other_meta_ref, absent) in enumerate(near):
            columns = pl.ds(number * OBS_BLOCK, OBS_BLOCK)
            value = jnp.where(me_ref[0] != absent, coupling(other_ref, other_meta_ref), 0.0)
            near_high_ref[rows, columns], near_low_ref[rows, columns] = split(value)


def product(left_ref, right):
    return jnp.dot(left_ref[...], right, preferred_element_type=jnp.float32)


def own_start_kernel(high_ref, low_ref, weights_ref, part_ref):
    high, low = split(weights_ref[...])
    part_ref[...] = product(high_ref, high) + product(low_ref, high) + product(high_ref, low)


def sweep_kernel(high_ref, low_ref, before_ref, after_ref, start_ref, part_ref, weights_ref, step_ref, rest_ref):
    high, low = split(jnp.concatenate([before_ref[...], after_ref[...]], axis=0))
    change = part_ref[...] + product(high_ref, high) + product(low_ref, high) + product(high_ref, low)
    weights_ref[...] = start_ref[...] + change
    step_ref[...], rest_ref[...] = split(change)


def own_step_kernel(high_ref, low_ref, step_ref, rest_ref, weights_ref, part_ref):
    step = step_ref[...]
    part_ref[...] = (
        weights_ref[...] + product(high_ref, step) + product(low_ref, step) + product(high_ref, rest_ref[...])
    )


def answer_kernel(high_ref, low_ref, before_ref, after_ref, part_ref, gain_ref, answer_ref):
    step = jnp.concatenate([before_ref[...], after_ref[...]], axis=0)
    weights = part_ref[...] + product(high_ref, step) + product(low_ref, step)
    answer_ref[...] = product(gain_ref, weights.astype(jnp.bfloat16))


def gain_kernel(inverse, rows_ref, slabs_ref, y_ref, meta_ref, gain_ref, product_ref):
    product_ref[...] = lax.dot_general(
        rows_ref[...], y_ref[...], (((1,), (1,)), ((), ())), preferred_element_type=jnp.float32
    )
    lines = slabs_ref.shape[2]
    height = CAP * lines
    here = as_row(meta_ref, 0)

    def group(number, carry):
        places = slabs_ref[number, CAP].astype(jnp.float32)
        scales = []
        for slot in range(CAP):
            place = places[2 * slot : 2 * slot + 1, :LANES] * 256.0 + places[2 * slot + 1 : 2 * slot + 2, :LANES]
            spread = (jnp.concatenate([place] * PARTS, axis=1) - here) * (1.0 / LENGTH)
            scale = inverse / (1.0 + spread * spread)
            scales.append(jnp.broadcast_to(scale, (lines, OBS_BLOCK)))
        source = pl.ds(pl.multiple_of(number * (CAP + 1) * lines, lines), height)
        rows = pl.ds(pl.multiple_of(number * height, height), height)
        gain = product_ref[source, :] * jnp.concatenate(scales, axis=0)
        gain_ref[rows, :] = gain.astype(jnp.bfloat16)
        return carry

    lax.fori_loop(0, slabs_ref.shape[0], group, 0, unroll=4)


def request_kernel(home_ref, reads_ref, place_ref, prior_ref, send_ref, slot_ref, count_ref, at_ref):
    tiles, lines, members = prior_ref.shape
    devices = send_ref.shape[0]
    send_ref[...] = jnp.zeros_like(send_ref)

    def clear(number, carry):
        for slot in range(CAP):
            at_ref[number * CAP + slot] = 0
        count_ref[number] = 0
        return carry

    lax.fori_loop(0, devices, clear, 0)

    def tile(number, carry):
        states = prior_ref[number].astype(jnp.float32)
        mean = jnp.sum(states, axis=1, keepdims=True) * (1.0 / members)
        anomalies = (states - mean).astype(send_ref.dtype)
        for read in range(READS):
            block = home_ref[reads_ref[number, read]]
            used = jnp.minimum(count_ref[block], CAP - 1)
            count_ref[block] = used + 1
            send_ref[block, used] = anomalies
            at_ref[block * CAP + used] = place_ref[number]
            slot_ref[number * READS + read] = block * CAP + used
        return carry

    lax.fori_loop(0, tiles, tile, 0)
    line = lax.broadcasted_iota(jnp.int32, (lines, members), 0)

    def place(number, carry):
        value = jnp.zeros((lines, members), jnp.int32)
        for slot in range(CAP):
            at = at_ref[number * CAP + slot]
            value = jnp.where(line == 2 * slot, at // 256, value)
            value = jnp.where(line == 2 * slot + 1, at % 256, value)
        send_ref[number, CAP] = value.astype(jnp.float32).astype(send_ref.dtype)
        return carry

    lax.fori_loop(0, devices, place, 0)


def collect_kernel(slot_ref, prior_ref, returned_ref, out_ref):
    def tile(number, carry):
        total = returned_ref[slot_ref[number * READS]]
        for read in range(1, READS):
            total = total + returned_ref[slot_ref[number * READS + read]]
        out_ref[number] = prior_ref[number].astype(jnp.float32) + total
        return carry

    lax.fori_loop(0, prior_ref.shape[0], tile, 0)


VMEM = pl.BlockSpec(memory_space=pltpu.VMEM)
SMEM = pl.BlockSpec(memory_space=pltpu.SMEM)


def call(kernel, ins, outs, scratch=()):
    shapes = [jax.ShapeDtypeStruct(shape, dtype) for shape, dtype, _ in outs]
    specs = [space for _, _, space in outs]
    single = len(outs) == 1
    return pl.pallas_call(
        kernel,
        in_specs=list(ins),
        out_shape=shapes[0] if single else shapes,
        out_specs=specs[0] if single else specs,
        scratch_shapes=list(scratch),
    )


def shards(
    home,
    prior_states,
    patch_mesh_location,
    fetched_blocks,
    measured_deviations,
    departure_vectors,
    measurement_error_spread,
    measurement_mesh_location,
):
    f32, bf16, i32 = jnp.float32, jnp.bfloat16, jnp.int32
    tiles, lines, members = prior_states.shape
    inverse = 1.0 / (members - 1)
    devices = len(home)
    slots = devices * CAP
    rows = slots * lines
    after = home[1:] + home[:1]
    before = home[-1:] + home[:-1]
    source = list(range(devices))
    up, down = list(zip(home, after)), list(zip(home, before))

    def send(values, pairs):
        return lax.ppermute(values, AXES, pairs)

    square = (OBS_BLOCK, members)
    y = send(measured_deviations, list(zip(source, home)))
    start, meta_here = call(
        functools.partial(start_kernel, inverse), [VMEM] * 4,
        [(square, f32, VMEM), ((2 * PARTS, LANES), f32, VMEM)],
    )(
        measured_deviations,
        measurement_mesh_location.reshape(PARTS, LANES),
        measurement_error_spread.reshape(PARTS, LANES),
        departure_vectors,
    )
    start = send(start, list(zip(source, home)))
    meta = send(meta_here, list(zip(source, home)))
    meta_before = send(meta_here, list(zip(source, after)))
    meta_after = send(meta_here, list(zip(source, before)))
    slabs = (devices, CAP + 1, lines, members)
    send_rows, slot = call(
        request_kernel,
        [SMEM, SMEM, SMEM, VMEM],
        [(slabs, bf16, VMEM), ((tiles * READS,), i32, SMEM)],
        [pltpu.SMEM((devices,), i32), pltpu.SMEM((slots,), i32)],
    )(jnp.asarray(home, i32), fetched_blocks, patch_mesh_location, prior_states)
    y_before, y_after = send(y, up), send(y, down)

    me = lax.axis_index(AXES).astype(i32).reshape(1)
    own_square, near_wide = (OBS_BLOCK, OBS_BLOCK), (OBS_BLOCK, 2 * OBS_BLOCK)
    own_high, own_low, near_high, near_low = call(
        functools.partial(couple_kernel, inverse, home[0], home[-1]),
        [SMEM] + [VMEM] * 6,
        [(own_square, bf16, VMEM)] * 2 + [(near_wide, bf16, VMEM)] * 2,
    )(me, y, y_before, y_after, meta, meta_before, meta_after)
    w_before, w_after = send(start, up), send(start, down)
    part = call(own_start_kernel, [VMEM] * 3, [(square, f32, VMEM)])(own_high, own_low, start)
    arrived = lax.all_to_all(send_rows, AXES, 0, 0, tiled=True)
    weights, step, rest = call(
        sweep_kernel, [VMEM] * 6,
        [(square, f32, VMEM), (square, bf16, VMEM), (square, bf16, VMEM)],
    )(near_high, near_low, w_before, w_after, start, part)
    step_before, step_after = send(step, up), send(step, down)
    part = call(own_step_kernel, [VMEM] * 5, [(square, f32, VMEM)])(
        own_high, own_low, step, rest, weights
    )
    gain = call(
        functools.partial(gain_kernel, inverse),
        [VMEM] * 4,
        [((rows, OBS_BLOCK), bf16, VMEM)],
        [pltpu.VMEM((devices * (CAP + 1) * lines, OBS_BLOCK), f32)],
    )(arrived.reshape(-1, members), arrived, y, meta)
    answers = call(answer_kernel, [VMEM] * 6, [((rows, members), f32, VMEM)])(
        near_high, near_low, step_before, step_after, part, gain
    )
    size = jnp.sqrt(jnp.abs(answers)) * (1.0 / 16)
    coded = jnp.where(answers < 0, -size, size).astype(jnp.float16)
    returned = lax.all_to_all(
        coded.reshape(devices, CAP, lines, members), AXES, 0, 0, tiled=True
    ).astype(f32)
    returned = returned * jnp.abs(returned) * 256.0
    return call(collect_kernel, [SMEM, VMEM, VMEM], [((tiles, lines, members), f32, VMEM)])(
        slot, prior_states, returned.reshape(slots, lines, members)
    )


def solution(mesh):
    atm, ocn = mesh.shape["atm"], mesh.shape["ocn"]
    home = homes(atm, ocn) if RELOCATE else list(range(atm * ocn))
    placed = (
        P(AXES, None, None),
        P(AXES),
        P(AXES, None),
        P(AXES, None),
        P(AXES, None),
        P(AXES),
        P(AXES),
    )

    def body(*arrays):
        return shards(home, *arrays)

    return jax.shard_map(
        body,
        mesh=mesh,
        in_specs=placed,
        out_specs=P(AXES, None, None),
        check_vma=False,
    )
```

time: 115 us -> 104 us (0.904)
  blocking collectives: 28.2 us -> 14.9 us
  starting transfers between devices: 29.9 us -> 40.9 us
  waiting for transfers between devices: 20 us -> 13.2 us
  Pallas kernels: 23.4 us -> 27.9 us
  local copies, waits for them, and re-layouts: 8.34 us -> 3.97 us
  other arithmetic: 3.83 us -> 2.18 us
    all_to_all x2 -> x1, blocking collectives: 28.2 us -> 14.9 us  [shards(): lax.all_to_all(coded.reshape(devices, CAP, lines, members), AXES, 0, 0, t...]
    ppermute x11, starting transfers between devices: 27 us -> 35.8 us  [send(): return lax.ppermute(values, AXES, pairs)]
    all_to_all x1, waiting for transfers between devices: 8.75 us -> 0.01 us  [shards(): arrived = lax.all_to_all(send_rows, AXES, 0, 0, tiled=True)]
    pallas_call x6 -> x8, Pallas kernels: 21.6 us -> 26.1 us  [the longest x1 4.28 us: shards(): call(functools.partial(couple_kernel, inverse, home[0], home[-1]), [SMEM]...]
    all_to_all x1, starting transfers between devices: 2.93 us -> 5.15 us  [shards(): arrived = lax.all_to_all(send_rows, AXES, 0, 0, tiled=True)]
    concatenate x2 -> x0, other arithmetic: 1.96 us -> none  [shards(): jnp.concatenate([measurement_mesh_location.astype(f32), measurement_error...]
    reshape x3 -> x0, local copies, waits for them, and re-layouts: 1.94 us -> none  [the longest x1 0.75 us: shards(): send_places.reshape(devices, 1, CAP)]
    ppermute x11, waiting for transfers between devices: 11.3 us -> 13.2 us  [send(): return lax.ppermute(values, AXES, pairs)]
  transfers between devices with their start and end apart: 12 -> 12, of which waited for: 5 -> 4; matrix products, arithmetic and copies ran while one was open for 5% -> 0% of each run, Pallas kernels for 8% -> 19%
where the time goes in v2:
time: 104 us; the launch traced here: 103 us
  starting transfers between devices  40.9 us (39%)
  Pallas kernels  27.9 us (27%)
  blocking collectives  14.9 us (14%)
  waiting for transfers between devices  13.2 us (13%)
  local copies, waits for them, and re-layouts  3.97 us (4%)
  other arithmetic  2.18 us (2%)
    ppermute x11, starting transfers between devices, send(): return lax.ppermute(values, AXES, pairs)  35.8 us
    all_to_all x1, blocking collectives, shards(): lax.all_to_all(coded.reshape(devices, CAP, lines, members), AXES, 0, 0, t...  14.9 us
    ppermute x11, waiting for transfers between devices, send(): return lax.ppermute(values, AXES, pairs)  13.2 us
    all_to_all x1, starting transfers between devices, shards(): arrived = lax.all_to_all(send_rows, AXES, 0, 0, tiled=True)  5.15 us
    pallas_call x1, Pallas kernels, shards(): call(functools.partial(couple_kernel, inverse, home[0], home[-1]), [SMEM]...  4.28 us
    pallas_call x1, Pallas kernels, shards(): call(sweep_kernel, [VMEM] * 6, [(square, f32, VMEM), (square, bf16, VMEM)...  4.11 us
    unnamed x28, local copies, waits for them, and re-layouts  3.97 us
    pallas_call x1, Pallas kernels, shards(): call(answer_kernel, [VMEM] * 6, [((rows, members), f32, VMEM)])  3.96 us
  transfers between devices with their start and end apart: 12, of which 4 were waited for; matrix products, arithmetic and copies ran while one was open for 0% of the time, Pallas kernels for 19%

profile of v2, /device:TPU:1, one launch (start us, length us, event | category | flops | bytes accessed | tf_op | source)
XLA Modules:
  0.0 103.3 jit_solution(6959266648265304204)
XLA Ops:
  0.0 0.0 copy-start.5
  0.0 2.2 %shard_map.83 = (f32[512,256]{1,0:T(8,128)}, f32[8,128]{1,0:T(8,128)}) custom-call(bf16[512,256]{1,0:T(8,128)(2,1)} %y_ref.1, s32[4,128]{1,0:T(4,128)} %bitcast.9, f32[4,128]{1,0:T(4,128)} %bitcast.10, f32[512,256]{1,0:T(8,128)} %target_ref.1), custom_call_target="tpu_custom_call" | custom-call | tf_op jit(solution)/shard_map/pallas_call | solution.py:235
  2.2 5.6 %collective-permute-start.6 = (f32[512,256]{1,0:T(8,128)}, f32[512,256]{1,0:T(8,128)S(1)}, u32[]{:S(2)}, u32[]{:S(2)}) collective-permute-start(f32[512,256]{1,0:T(8,128)} %get-tuple-element.20), channel_id=1, source_target_pairs={{0,0},{1,4},{2,1},{3,5},{4,2},{5,6},{6,3},{7,7},{8,11},{9,15},{10,... | collective-permute-start | bytes 1572872 | tf_op jit(solution)/shard_map/ppermute | solution.py:231
  7.8 0.0 copy-done.5
  7.8 2.4 %collective-permute-start = (bf16[512,256]{1,0:T(8,128)(2,1)S(1)}, bf16[512,256]{1,0:T(8,128)(2,1)S(1)}, u32[]{:S(2)}, u32[]{:S(2)}) collective-permute-start(bf16[512,256]{1,0:T(8,128)(2,1)S(1)} %copy-done.5), channel_id=1, source_target_pairs={{0,0},{1,4},{2,1},{3,5},{4,2},{5,6},{6,3},{7,7},{8,11},{9,15},{10,... | collective-permute-start | bytes 786440 | tf_op jit(solution)/shard_map/ppermute | solution.py:231
  10.2 4.1 %collective-permute-done.6.weights_ref.start_ref = f32[512,256]{1,0:T(8,128)S(1)} collective-permute-done((f32[512,256]{1,0:T(8,128)}, f32[512,256]{1,0:T(8,128)S(1)}, u32[]{:S(2)}, u32[]{:S(2)}) %collective-permute-start.6) | collective-permute-done | bytes 524320 | tf_op jit(solution)/shard_map/ppermute | solution.py:231
  14.3 0.0 copy-start.1
  14.3 10.3 %collective-permute-start.7 = (f32[512,256]{1,0:T(8,128)S(1)}, f32[512,256]{1,0:T(8,128)S(1)}, u32[]{:S(2)}, u32[]{:S(2)}) collective-permute-start(f32[512,256]{1,0:T(8,128)S(1)} %collective-permute-done.6.weights_ref.start_ref), channel_id=1, source_target_pairs={{0,4},{4,1},{1,5},{5,2},{2,6},{6,3},{3,7},{7,11},{11,15},{15,10},{... | collective-permute-start | bytes 1572872 | tf_op jit(solution)/shard_map/ppermute | solution.py:231
  24.6 0.0 collective-permute-start.8
  24.6 3.1 %shard_map.82 = (bf16[32,3,8,256]{3,2,1,0:T(8,128)(2,1)}, s32[40]{0:T(128)}) custom-call(s32[32]{0:T(128)} %constant.19.clone.home_ref, s32[8,5]{1,0:T(8,128)} %reads_ref.1, s32[8]{0:T(128)} %place_ref.1, bf16[8,8,256]{2,1,0:T(8,128)(2,1)} %prior_ref.3), custom_call_target="tpu_custom_call" | custom-call | tf_op jit(solution)/shard_map/pallas_call | solution.py:249
  27.7 0.0 copy-start.13
  27.7 5.1 %all-to-all-start = ((bf16[32,3,8,256]{3,2,1,0:T(8,128)(2,1)}), bf16[32,3,8,256]{3,2,1,0:T(8,128)(2,1)S(1)}, u32[]{:S(2)}, u32[]{:S(2)}) async-start(bf16[32,3,8,256]{3,2,1,0:T(8,128)(2,1)} %get-tuple-element.26), calls=%async_computation | async-start | bytes 786432 | tf_op jit(solution)/shard_map/all_to_all | solution.py:266
  32.9 0.0 collective-permute-done.y_ref
  32.9 0.0 copy-start.2
  32.9 1.7 %collective-permute-start.1 = (bf16[512,256]{1,0:T(8,128)(2,1)S(1)}, bf16[512,256]{1,0:T(8,128)(2,1)S(1)}, u32[]{:S(2)}, u32[]{:S(2)}) collective-permute-start(bf16[512,256]{1,0:T(8,128)(2,1)S(1)} %collective-permute-done.y_ref), channel_id=1, source_target_pairs={{0,4},{4,1},{1,5},{5,2},{2,6},{6,3},{3,7},{7,11},{11,15},{15,10},{... | collective-permute-start | bytes 786440 | tf_op jit(solution)/shard_map/ppermute | solution.py:231
  34.6 0.0 collective-permute-start.2
  34.6 0.0 copy-done.13
  34.6 4.5 %collective-permute-start.3 = (f32[8,128]{1,0:T(8,128)S(1)}, f32[8,128]{1,0:T(8,128)S(1)}, u32[]{:S(2)}, u32[]{:S(2)}) collective-permute-start(f32[8,128]{1,0:T(8,128)S(1)} %copy-done.13), channel_id=1, source_target_pairs={{0,0},{1,4},{2,1},{3,5},{4,2},{5,6},{6,3},{7,7},{8,11},{9,15},{10,... | collective-permute-start | bytes 12296 | tf_op jit(solution)/shard_map/ppermute | solution.py:231
  39.1 5.5 %collective-permute-done.3.meta_ref = f32[8,128]{1,0:T(8,128)S(1)} collective-permute-done((f32[8,128]{1,0:T(8,128)S(1)}, f32[8,128]{1,0:T(8,128)S(1)}, u32[]{:S(2)}, u32[]{:S(2)}) %collective-permute-start.3) | collective-permute-done | bytes 4128 | tf_op jit(solution)/shard_map/ppermute | solution.py:231
  44.6 0.0 copy-start.10
  44.6 5.3 %collective-permute-start.4 = (f32[8,128]{1,0:T(8,128)S(1)}, f32[8,128]{1,0:T(8,128)S(1)}, u32[]{:S(2)}, u32[]{:S(2)}) collective-permute-start(f32[8,128]{1,0:T(8,128)S(1)} %copy-done.13), channel_id=1, source_target_pairs={{0,4},{1,1},{2,5},{3,2},{4,6},{5,3},{6,7},{7,11},{8,15},{9,10},{10... | collective-permute-start | bytes 12296 | tf_op jit(solution)/shard_map/ppermute | solution.py:231
  49.9 0.7 collective-permute-done.4.meta_before_ref
  50.6 0.0 copy-start.11
  50.6 2.9 %collective-permute-start.5 = (f32[8,128]{1,0:T(8,128)S(1)}, f32[8,128]{1,0:T(8,128)S(1)}, u32[]{:S(2)}, u32[]{:S(2)}) collective-permute-start(f32[8,128]{1,0:T(8,128)S(1)} %copy-done.13), channel_id=1, source_target_pairs={{0,28},{1,0},{2,4},{3,1},{4,5},{5,2},{6,6},{7,3},{8,7},{9,11},{10,... | collective-permute-start | bytes 12296 | tf_op jit(solution)/shard_map/ppermute | solution.py:231
  53.5 0.0 copy-done.10
  53.5 0.0 copy-done.11
  53.5 2.9 %collective-permute-done.5.meta_after_ref = f32[8,128]{1,0:T(8,128)S(1)} collective-permute-done((f32[8,128]{1,0:T(8,128)S(1)}, f32[8,128]{1,0:T(8,128)S(1)}, u32[]{:S(2)}, u32[]{:S(2)}) %collective-permute-start.5) | collective-permute-done | bytes 4128 | tf_op jit(solution)/shard_map/ppermute | solution.py:231
  56.5 0.0 copy-start.12
  56.5 0.0 collective-permute-done.1.before_ref
  56.5 0.0 copy-start.8
  56.5 0.0 collective-permute-done.2.after_ref
  56.5 0.0 copy-start.9
  56.5 0.0 copy-done.2
  56.5 0.6 copy-done.12
  57.0 0.1 copy-done.8
  57.2 0.1 copy-done.9
  57.3 4.3 %shard_map.84 = (bf16[512,512]{1,0:T(8,128)(2,1)}, bf16[512,512]{1,0:T(8,128)(2,1)}, bf16[512,1024]{1,0:T(8,128)(2,1)}, bf16[512,1024]{1,0:T(8,128)(2,1)}) custom-call(s32[1]{0:T(128)} %bitcast.me_ref, bf16[512,256]{1,0:T(8,128)(2,1)} %copy-done.2, bf16[512,256]{1,0:T(8,128)(2,1)} %copy-done.8, bf16[512,256]{1,0:T(8,128)(2,1)} %copy-done.9, ...), custom_call_target="tpu_custom_call" | custom-call | tf_op jit(solution)/shard_map/pallas_call | solution.py:259
  61.5 0.0 copy-done.1
  61.5 2.7 %shard_map.85.part_ref = f32[512,256]{1,0:T(8,128)} custom-call(bf16[512,512]{1,0:T(8,128)(2,1)} %get-tuple-element.21.high_ref, bf16[512,512]{1,0:T(8,128)(2,1)} %get-tuple-element.22.low_ref, f32[512,256]{1,0:T(8,128)} %copy-done.1), custom_call_target="tpu_custom_call" | custom-call | tf_op jit(solution)/shard_map/pallas_call | solution.py:265
  64.3 0.0 collective-permute-done.7.before_ref
  64.3 0.0 copy-start.3
  64.3 0.0 collective-permute-done.8.after_ref
  64.3 0.0 copy-start.4
  64.3 0.8 copy-done.3
  65.1 0.2 copy-done.4
  65.3 4.1 %shard_map.86 = (f32[512,256]{1,0:T(8,128)}, bf16[512,256]{1,0:T(8,128)(2,1)}, bf16[512,256]{1,0:T(8,128)(2,1)}) custom-call(bf16[512,1024]{1,0:T(8,128)(2,1)} %get-tuple-element.18.high_ref, bf16[512,1024]{1,0:T(8,128)(2,1)} %get-tuple-element.19.low_ref, f32[512,256]{1,0:T(8,128)} %copy-done.3, f32[512,256]{1,0:T(8,128)} %copy-done.4, ...), custom_call_target="tpu_custom_call" | custom-call | tf_op jit(solution)/shard_map/pallas_call | solution.py:267
  69.4 3.1 %collective-permute-start.10 = (bf16[512,256]{1,0:T(8,128)(2,1)}, bf16[512,256]{1,0:T(8,128)(2,1)S(1)}, u32[]{:S(2)}, u32[]{:S(2)}) collective-permute-start(bf16[512,256]{1,0:T(8,128)(2,1)} %get-tuple-element.23.step_ref), channel_id=1, source_target_pairs={{0,28},{4,0},{1,4},{5,1},{2,5},{6,2},{3,6},{7,3},{11,7},{15,11},{1... | collective-permute-start | bytes 786440 | tf_op jit(solution)/shard_map/ppermute | solution.py:231
  72.5 0.0 collective-permute-start.9
  72.5 0.0 all-to-all-done.slabs_ref
  72.5 0.0 copy-start
  72.5 0.8 copy-done
  73.3 2.8 %shard_map.88.gain_ref = bf16[512,512]{1,0:T(8,128)(2,1)} custom-call(bf16[768,256]{1,0:T(8,128)(2,1)} %bitcast.6, bf16[32,3,8,256]{3,2,1,0:T(8,128)(2,1)} %copy-done, bf16[512,256]{1,0:T(8,128)(2,1)} %copy-done.2, f32[8,128]{1,0:T(8,128)} %copy-done.10), custom_call_target="tpu_custom_call" | custom-call | tf_op jit(solution)/shard_map/pallas_call | solution.py:275
  76.1 2.9 %shard_map.87.part_ref = f32[512,256]{1,0:T(8,128)} custom-call(bf16[512,512]{1,0:T(8,128)(2,1)} %get-tuple-element.21.high_ref, bf16[512,512]{1,0:T(8,128)(2,1)} %get-tuple-element.22.low_ref, bf16[512,256]{1,0:T(8,128)(2,1)} %get-tuple-element.23.step_ref, bf16[512,256]{1,0:T(8,128)(2,1)} %get-tuple-element.24.rest_ref, ...), custom_call_target="tpu_custom_call" | custom-call | tf_op jit(solution)/shard_map/pallas_call | solution.py:272
  79.0 0.0 collective-permute-done.10.after_ref
  79.0 0.0 copy-start.6
  79.0 0.0 collective-permute-done.9.before_ref
  79.0 0.7 copy-done.6
  79.7 0.0 copy-start.7
  79.7 0.7 copy-done.7
  80.4 4.0 %shard_map.89 = f32[512,256]{1,0:T(8,128)} custom-call(bf16[512,1024]{1,0:T(8,128)(2,1)} %get-tuple-element.18.high_ref, bf16[512,1024]{1,0:T(8,128)(2,1)} %get-tuple-element.19.low_ref, bf16[512,256]{1,0:T(8,128)(2,1)} %copy-done.7, bf16[512,256]{1,0:T(8,128)(2,1)} %copy-done.6, f32[512,256]{1,0:T(8,128)} %shard_map.87.part_ref, ...), custom_call_target="tpu_custom_call" | custom-call | tf_op jit(solution)/shard_map/pallas_call | solution.py:281
  84.3 1.3 %fusion = f16[512,256]{1,0:T(8,128)(2,1)S(1)} fusion(f32[512,256]{1,0:T(8,128)} %shard_map.89), kind=kLoop, calls=%fused_computation.2 | loop fusion | flops 786432 | bytes 786432 | tf_op jit(solution)/shard_map/convert_element_type | solution.py:285
  85.6 14.9 %all_to_all.10 = f16[32,2,8,256]{3,2,1,0:T(8,128)(2,1)S(1)} all-to-all(f16[32,2,8,256]{3,2,1,0:T(8,128)(2,1)S(1)} %bitcast.8), channel_id=1, replica_groups=mesh['atm'=8,'ocn'=4] {'atm','ocn'}, dimensions={0} | all-to-all | bytes 524288 | tf_op jit(solution)/shard_map/all_to_all | solution.py:286
  100.6 0.9 fusion.1
  101.5 1.8 %shard_map.90 = f32[8,8,256]{2,1,0:T(8,128)} custom-call(s32[40]{0:T(128)} %get-tuple-element.16.slot_ref, bf16[8,8,256]{2,1,0:T(8,128)(2,1)} %prior_ref.3, f32[64,8,256]{2,1,0:T(8,128)} %bitcast.7), custom_call_target="tpu_custom_call" | custom-call | tf_op jit(solution)/shard_map/pallas_call | solution.py:290
Async XLA Ops:
  0.0 7.8 %copy-start.5 = (bf16[512,256]{1,0:T(8,128)(2,1)S(1)}, bf16[512,256]{1,0:T(8,128)(2,1)}, u32[]{:S(2)}) copy-start(bf16[512,256]{1,0:T(8,128)(2,1)} %y_ref.1) | copy-start | bytes 786436
  2.2 12.1 %collective-permute-start.6 = (f32[512,256]{1,0:T(8,128)}, f32[512,256]{1,0:T(8,128)S(1)}, u32[]{:S(2)}, u32[]{:S(2)}) collective-permute-start(f32[512,256]{1,0:T(8,128)} %get-tuple-element.20), channel_id=1, source_target_pairs={{0,0},{1,4},{2,1},{3,5},{4,2},{5,6},{6,3},{7,7},{8,11},{9,15},{10,... | collective-permute-start | bytes 1572872 | tf_op jit(solution)/shard_map/ppermute | solution.py:231
  7.8 25.0 %collective-permute-start = (bf16[512,256]{1,0:T(8,128)(2,1)S(1)}, bf16[512,256]{1,0:T(8,128)(2,1)S(1)}, u32[]{:S(2)}, u32[]{:S(2)}) collective-permute-start(bf16[512,256]{1,0:T(8,128)(2,1)S(1)} %copy-done.5), channel_id=1, source_target_pairs={{0,0},{1,4},{2,1},{3,5},{4,2},{5,6},{6,3},{7,7},{8,11},{9,15},{10,... | collective-permute-start | bytes 786440 | tf_op jit(solution)/shard_map/ppermute | solution.py:231
  14.3 47.2 %copy-start.1 = (f32[512,256]{1,0:T(8,128)}, f32[512,256]{1,0:T(8,128)S(1)}, u32[]{:S(2)}) copy-start(f32[512,256]{1,0:T(8,128)S(1)} %collective-permute-done.6.weights_ref.start_ref) | copy-start | bytes 1572868
  14.3 50.0 %collective-permute-start.7 = (f32[512,256]{1,0:T(8,128)S(1)}, f32[512,256]{1,0:T(8,128)S(1)}, u32[]{:S(2)}, u32[]{:S(2)}) collective-permute-start(f32[512,256]{1,0:T(8,128)S(1)} %collective-permute-done.6.weights_ref.start_ref), channel_id=1, source_target_pairs={{0,4},{4,1},{1,5},{5,2},{2,6},{6,3},{3,7},{7,11},{11,15},{15,10},{... | collective-permute-start | bytes 1572872 | tf_op jit(solution)/shard_map/ppermute | solution.py:231
  24.6 39.7 %collective-permute-start.8 = (f32[512,256]{1,0:T(8,128)S(1)}, f32[512,256]{1,0:T(8,128)S(1)}, u32[]{:S(2)}, u32[]{:S(2)}) collective-permute-start(f32[512,256]{1,0:T(8,128)S(1)} %collective-permute-done.6.weights_ref.start_ref), channel_id=1, source_target_pairs={{0,28},{4,0},{1,4},{5,1},{2,5},{6,2},{3,6},{7,3},{11,7},{15,11},{1... | collective-permute-start | bytes 1572872 | tf_op jit(solution)/shard_map/ppermute | solution.py:231
  27.7 6.9 %copy-start.13 = (f32[8,128]{1,0:T(8,128)S(1)}, f32[8,128]{1,0:T(8,128)}, u32[]{:S(2)}) copy-start(f32[8,128]{1,0:T(8,128)} %get-tuple-element.17) | copy-start | bytes 12292
  27.7 44.8 %all-to-all-start = ((bf16[32,3,8,256]{3,2,1,0:T(8,128)(2,1)}), bf16[32,3,8,256]{3,2,1,0:T(8,128)(2,1)S(1)}, u32[]{:S(2)}, u32[]{:S(2)}) async-start(bf16[32,3,8,256]{3,2,1,0:T(8,128)(2,1)} %get-tuple-element.26), calls=%async_computation | async-start | bytes 786432 | tf_op jit(solution)/shard_map/all_to_all | solution.py:266
  32.9 23.6 %copy-start.2 = (bf16[512,256]{1,0:T(8,128)(2,1)}, bf16[512,256]{1,0:T(8,128)(2,1)S(1)}, u32[]{:S(2)}) copy-start(bf16[512,256]{1,0:T(8,128)(2,1)S(1)} %collective-permute-done.y_ref) | copy-start | bytes 786436
  32.9 23.6 %collective-permute-start.1 = (bf16[512,256]{1,0:T(8,128)(2,1)S(1)}, bf16[512,256]{1,0:T(8,128)(2,1)S(1)}, u32[]{:S(2)}, u32[]{:S(2)}) collective-permute-start(bf16[512,256]{1,0:T(8,128)(2,1)S(1)} %collective-permute-done.y_ref), channel_id=1, source_target_pairs={{0,4},{4,1},{1,5},{5,2},{2,6},{6,3},{3,7},{7,11},{11,15},{15,10},{... | collective-permute-start | bytes 786440 | tf_op jit(solution)/shard_map/ppermute | solution.py:231
  34.6 21.9 %collective-permute-start.2 = (bf16[512,256]{1,0:T(8,128)(2,1)S(1)}, bf16[512,256]{1,0:T(8,128)(2,1)S(1)}, u32[]{:S(2)}, u32[]{:S(2)}) collective-permute-start(bf16[512,256]{1,0:T(8,128)(2,1)S(1)} %collective-permute-done.y_ref), channel_id=1, source_target_pairs={{0,28},{4,0},{1,4},{5,1},{2,5},{6,2},{3,6},{7,3},{11,7},{15,11},{1... | collective-permute-start | bytes 786440 | tf_op jit(solution)/shard_map/ppermute | solution.py:231
  34.6 10.0 %collective-permute-start.3 = (f32[8,128]{1,0:T(8,128)S(1)}, f32[8,128]{1,0:T(8,128)S(1)}, u32[]{:S(2)}, u32[]{:S(2)}) collective-permute-start(f32[8,128]{1,0:T(8,128)S(1)} %copy-done.13), channel_id=1, source_target_pairs={{0,0},{1,4},{2,1},{3,5},{4,2},{5,6},{6,3},{7,7},{8,11},{9,15},{10,... | collective-permute-start | bytes 12296 | tf_op jit(solution)/shard_map/ppermute | solution.py:231
  44.6 8.9 %copy-start.10 = (f32[8,128]{1,0:T(8,128)}, f32[8,128]{1,0:T(8,128)S(1)}, u32[]{:S(2)}) copy-start(f32[8,128]{1,0:T(8,128)S(1)} %collective-permute-done.3.meta_ref) | copy-start | bytes 12292
  44.6 6.0 %collective-permute-start.4 = (f32[8,128]{1,0:T(8,128)S(1)}, f32[8,128]{1,0:T(8,128)S(1)}, u32[]{:S(2)}, u32[]{:S(2)}) collective-permute-start(f32[8,128]{1,0:T(8,128)S(1)} %copy-done.13), channel_id=1, source_target_pairs={{0,4},{1,1},{2,5},{3,2},{4,6},{5,3},{6,7},{7,11},{8,15},{9,10},{10... | collective-permute-start | bytes 12296 | tf_op jit(solution)/shard_map/ppermute | solution.py:231
  50.6 2.9 %copy-start.11 = (f32[8,128]{1,0:T(8,128)}, f32[8,128]{1,0:T(8,128)S(1)}, u32[]{:S(2)}) copy-start(f32[8,128]{1,0:T(8,128)S(1)} %collective-permute-done.4.meta_before_ref) | copy-start | bytes 12292
  50.6 5.8 %collective-permute-start.5 = (f32[8,128]{1,0:T(8,128)S(1)}, f32[8,128]{1,0:T(8,128)S(1)}, u32[]{:S(2)}, u32[]{:S(2)}) collective-permute-start(f32[8,128]{1,0:T(8,128)S(1)} %copy-done.13), channel_id=1, source_target_pairs={{0,28},{1,0},{2,4},{3,1},{4,5},{5,2},{6,6},{7,3},{8,7},{9,11},{10,... | collective-permute-start | bytes 12296 | tf_op jit(solution)/shard_map/ppermute | solution.py:231
  56.5 0.6 copy-start.12
  56.5 0.7 copy-start.8
  56.5 0.8 copy-start.9
  64.3 0.8 copy-start.3
  64.3 1.0 copy-start.4
  69.4 9.6 %collective-permute-start.10 = (bf16[512,256]{1,0:T(8,128)(2,1)}, bf16[512,256]{1,0:T(8,128)(2,1)S(1)}, u32[]{:S(2)}, u32[]{:S(2)}) collective-permute-start(bf16[512,256]{1,0:T(8,128)(2,1)} %get-tuple-element.23.step_ref), channel_id=1, source_target_pairs={{0,28},{4,0},{1,4},{5,1},{2,5},{6,2},{3,6},{7,3},{11,7},{15,11},{1... | collective-permute-start | bytes 786440 | tf_op jit(solution)/shard_map/ppermute | solution.py:231
  72.5 6.5 %collective-permute-start.9 = (bf16[512,256]{1,0:T(8,128)(2,1)}, bf16[512,256]{1,0:T(8,128)(2,1)S(1)}, u32[]{:S(2)}, u32[]{:S(2)}) collective-permute-start(bf16[512,256]{1,0:T(8,128)(2,1)} %get-tuple-element.23.step_ref), channel_id=1, source_target_pairs={{0,4},{4,1},{1,5},{5,2},{2,6},{6,3},{3,7},{7,11},{11,15},{15,10},{... | collective-permute-start | bytes 786440 | tf_op jit(solution)/shard_map/ppermute | solution.py:231
  72.5 0.8 copy-start
  79.0 0.7 copy-start.6
  79.7 0.7 copy-start.7

commit v3 on v2

--- a/solution.py
+++ b/solution.py
@@ -14,6 +14,7 @@
 LENGTH = 16384
 LANES = 128
 PARTS = OBS_BLOCK // LANES
+EXTRA = 8
 AXES = ("atm", "ocn")
 RELOCATE = True
 
@@ -29,13 +30,18 @@
 
 
 def as_row(ref, start):
-    return jnp.concatenate([ref[start + i : start + i + 1, :] for i in range(PARTS)], axis=1)
+    return jnp.concatenate([ref[start + i : start + i + 1, :] for i in range(ref_rows(ref))], axis=1)
+
+
+def ref_rows(ref):
+    return OBS_BLOCK // ref.shape[1]
 
 
 def as_column(ref, start, part):
     shape = (LANES, LANES)
     diagonal = lax.broadcasted_iota(jnp.int32, shape, 0) == lax.broadcasted_iota(jnp.int32, shape, 1)
-    row = jnp.broadcast_to(ref[start + part : start + part + 1, :], shape)
+    line, lane = divmod(part * LANES, ref.shape[1])
+    row = jnp.broadcast_to(ref[start + line : start + line + 1, lane : lane + LANES], shape)
     return jnp.sum(jnp.where(diagonal, row, 0.0), axis=1, keepdims=True)
 
 
@@ -44,58 +50,65 @@
     return high, (values - high.astype(jnp.float32)).astype(jnp.bfloat16)
 
 
-def start_kernel(inverse, y_ref, place_ref, error_ref, target_ref, weights_ref, meta_ref):
-    meta_ref[:PARTS, :] = place_ref[...].astype(jnp.float32)
-    meta_ref[PARTS:, :] = error_ref[...]
+def start_kernel(inverse, y_ref, place_ref, error_ref, target_ref, weights_ref):
+    members = weights_ref.shape[1]
+    weights_ref[OBS_BLOCK:, :] = jnp.zeros((EXTRA, members), jnp.float32)
     for part in range(PARTS):
+        line, lane = divmod(part * LANES, members)
+        line, lanes = OBS_BLOCK + line, pl.ds(lane, LANES)
+        weights_ref[line : line + 1, lanes] = place_ref[part : part + 1, :].astype(jnp.float32)
+        line = line + OBS_BLOCK // members
+        weights_ref[line : line + 1, lanes] = error_ref[part : part + 1, :]
         rows = pl.ds(part * LANES, LANES)
         y = y_ref[rows, :].astype(jnp.float32)
         divisor = jnp.sum(y * y, axis=1, keepdims=True) * inverse + as_column(error_ref, 0, part)
         weights_ref[rows, :] = target_ref[rows, :] / divisor
 
 
-def couple_kernel(
-    inverse, first, last, me_ref, y_ref, before_ref, after_ref, meta_ref, meta_before_ref, meta_after_ref,
-    own_high_ref, own_low_ref, near_high_ref, near_low_ref,
+def coupling(inverse, part, y_ref, meta_ref, other_ref, other_meta_ref):
+    y = y_ref[pl.ds(part * LANES, LANES), :]
+    wide = y.astype(jnp.float32)
+    error = as_column(meta_ref, OBS_BLOCK + ref_rows(meta_ref), part)
+    divisor = jnp.sum(wide * wide, axis=1, keepdims=True) * inverse + error
+    product = lax.dot_general(
+        y, other_ref[...], (((1,), (1,)), ((), ())), preferred_element_type=jnp.float32
+    )
+    spread = (as_column(meta_ref, OBS_BLOCK, part) - as_row(other_meta_ref, OBS_BLOCK)) * (1.0 / LENGTH)
+    return product * (-inverse / (divisor * (1.0 + spread * spread)))
+
+
+def product(left_ref, right):
+    return jnp.dot(left_ref[...], right, preferred_element_type=jnp.float32)
+
+
+def own_kernel(inverse, y_ref, start_ref, high_ref, low_ref, part_ref, meta_ref):
+    for part in range(PARTS):
+        shape = (LANES, OBS_BLOCK)
+        line = lax.broadcasted_iota(jnp.int32, shape, 0) + part * LANES
+        value = coupling(inverse, part, y_ref, start_ref, y_ref, start_ref)
+        value = jnp.where(line == lax.broadcasted_iota(jnp.int32, shape, 1), 0.0, value)
+        rows = pl.ds(part * LANES, LANES)
+        high_ref[rows, :], low_ref[rows, :] = split(value)
+    meta_ref[...] = start_ref[OBS_BLOCK:, :]
+    high, low = split(start_ref[:OBS_BLOCK, :])
+    part_ref[...] = product(high_ref, high) + product(low_ref, high) + product(high_ref, low)
+
+
+def sweep_kernel(
+    inverse, first, last, me_ref, y_ref, y_before_ref, y_after_ref, start_ref, before_ref, after_ref, part_ref,
+    high_ref, low_ref, weights_ref, step_ref, rest_ref,
 ):
-    near = ((before_ref, meta_before_ref, first), (after_ref, meta_after_ref, last))
+    near = ((y_before_ref, before_ref, first), (y_after_ref, after_ref, last))
     for part in range(PARTS):
         rows = pl.ds(part * LANES, LANES)
-        y = y_ref[rows, :]
-        wide = y.astype(jnp.float32)
-        divisor = jnp.sum(wide * wide, axis=1, keepdims=True) * inverse + as_column(meta_ref, PARTS, part)
-        place = as_column(meta_ref, 0, part)
-
-        def coupling(other_ref, other_meta_ref):
-            product = lax.dot_general(
-                y, other_ref[...], (((1,), (1,)), ((), ())), preferred_element_type=jnp.float32
-            )
-            spread = (place - as_row(other_meta_ref, 0)) * (1.0 / LENGTH)
-            return product * (-inverse / (divisor * (1.0 + spread * spread)))
-
-        shape = (LANES, OBS_BLOCK)
-        line = lax.broadcasted_iota(jnp.int32, shape, 0) + part * LANES
-        own = jnp.where(line == lax.broadcasted_iota(jnp.int32, shape, 1), 0.0, coupling(y_ref, meta_ref))
-        own_high_ref[rows, :], own_low_ref[rows, :] = split(own)
         for number, (other_ref, other_meta_ref, absent) in enumerate(near):
             columns = pl.ds(number * OBS_BLOCK, OBS_BLOCK)
-            value = jnp.where(me_ref[0] != absent, coupling(other_ref, other_meta_ref), 0.0)
-            near_high_ref[rows, columns], near_low_ref[rows, columns] = split(value)
-
-
-def product(left_ref, right):
-    return jnp.dot(left_ref[...], right, preferred_element_type=jnp.float32)
-
-
-def own_start_kernel(high_ref, low_ref, weights_ref, part_ref):
-    high, low = split(weights_ref[...])
-    part_ref[...] = product(high_ref, high) + product(low_ref, high) + product(high_ref, low)
-
-
-def sweep_kernel(high_ref, low_ref, before_ref, after_ref, start_ref, part_ref, weights_ref, step_ref, rest_ref):
-    high, low = split(jnp.concatenate([before_ref[...], after_ref[...]], axis=0))
+            value = coupling(inverse, part, y_ref, start_ref, other_ref, other_meta_ref)
+            value = jnp.where(me_ref[0] != absent, value, 0.0)
+            high_ref[rows, columns], low_ref[rows, columns] = split(value)
+    high, low = split(jnp.concatenate([before_ref[:OBS_BLOCK, :], after_ref[:OBS_BLOCK, :]], axis=0))
     change = part_ref[...] + product(high_ref, high) + product(low_ref, high) + product(high_ref, low)
-    weights_ref[...] = start_ref[...] + change
+    weights_ref[...] = start_ref[:OBS_BLOCK, :] + change
     step_ref[...], rest_ref[...] = split(change)
 
 
@@ -189,21 +202,38 @@
     lax.fori_loop(0, prior_ref.shape[0], tile, 0)
 
 
-VMEM = pl.BlockSpec(memory_space=pltpu.VMEM)
-SMEM = pl.BlockSpec(memory_space=pltpu.SMEM)
+VMEM, SMEM, FAR, FREE = "vmem", "smem", "far", "free"
+SPECS = {
+    VMEM: pl.BlockSpec(memory_space=pltpu.VMEM),
+    SMEM: pl.BlockSpec(memory_space=pltpu.SMEM),
+    FAR: pl.BlockSpec(),
+    FREE: pl.BlockSpec(),
+}
 
 
 def call(kernel, ins, outs, scratch=()):
-    shapes = [jax.ShapeDtypeStruct(shape, dtype) for shape, dtype, _ in outs]
-    specs = [space for _, _, space in outs]
+    held = {VMEM: pltpu.VMEM, FAR: pltpu.HBM}
+    shapes = [held.get(space, jax.ShapeDtypeStruct)(shape, dtype) for shape, dtype, space in outs]
+    specs = [SPECS[space] for _, _, space in outs]
     single = len(outs) == 1
-    return pl.pallas_call(
+    run = pl.pallas_call(
         kernel,
-        in_specs=list(ins),
+        in_specs=[SPECS[space] for space in ins],
         out_shape=shapes[0] if single else shapes,
         out_specs=specs[0] if single else specs,
         scratch_shapes=list(scratch),
-    )
+        compiler_params=pltpu.CompilerParams(vmem_limit_bytes=24 << 20),
+    )
+
+    def on_chip(*operands):
+        return run(
+            *(
+                pltpu.with_memory_space_constraint(operand, held[space]) if space in held else operand
+                for operand, space in zip(operands, ins)
+            )
+        )
+
+    return on_chip
 
 
 def shards(
@@ -232,49 +262,41 @@
 
     square = (OBS_BLOCK, members)
     y = send(measured_deviations, list(zip(source, home)))
-    start, meta_here = call(
-        functools.partial(start_kernel, inverse), [VMEM] * 4,
-        [(square, f32, VMEM), ((2 * PARTS, LANES), f32, VMEM)],
-    )(
+    tall = (OBS_BLOCK + EXTRA, members)
+    start = call(functools.partial(start_kernel, inverse), [FAR, FREE, FREE, FAR], [(tall, f32, VMEM)])(
         measured_deviations,
         measurement_mesh_location.reshape(PARTS, LANES),
         measurement_error_spread.reshape(PARTS, LANES),
         departure_vectors,
     )
     start = send(start, list(zip(source, home)))
-    meta = send(meta_here, list(zip(source, home)))
-    meta_before = send(meta_here, list(zip(source, after)))
-    meta_after = send(meta_here, list(zip(source, before)))
     slabs = (devices, CAP + 1, lines, members)
     send_rows, slot = call(
         request_kernel,
         [SMEM, SMEM, SMEM, VMEM],
-        [(slabs, bf16, VMEM), ((tiles * READS,), i32, SMEM)],
+        [(slabs, bf16, FAR), ((tiles * READS,), i32, SMEM)],
         [pltpu.SMEM((devices,), i32), pltpu.SMEM((slots,), i32)],
     )(jnp.asarray(home, i32), fetched_blocks, patch_mesh_location, prior_states)
     y_before, y_after = send(y, up), send(y, down)
 
+    w_before, w_after = send(start, up), send(start, down)
     me = lax.axis_index(AXES).astype(i32).reshape(1)
     own_square, near_wide = (OBS_BLOCK, OBS_BLOCK), (OBS_BLOCK, 2 * OBS_BLOCK)
-    own_high, own_low, near_high, near_low = call(
-        functools.partial(couple_kernel, inverse, home[0], home[-1]),
-        [SMEM] + [VMEM] * 6,
-        [(own_square, bf16, VMEM)] * 2 + [(near_wide, bf16, VMEM)] * 2,
-    )(me, y, y_before, y_after, meta, meta_before, meta_after)
-    w_before, w_after = send(start, up), send(start, down)
-    part = call(own_start_kernel, [VMEM] * 3, [(square, f32, VMEM)])(own_high, own_low, start)
+    own_high, own_low, part, meta = call(
+        functools.partial(own_kernel, inverse), [VMEM] * 2,
+        [(own_square, bf16, FAR)] * 2 + [(square, f32, VMEM)] + [((EXTRA, members), f32, VMEM)],
+    )(y, start)
     arrived = lax.all_to_all(send_rows, AXES, 0, 0, tiled=True)
-    weights, step, rest = call(
-        sweep_kernel, [VMEM] * 6,
-        [(square, f32, VMEM), (square, bf16, VMEM), (square, bf16, VMEM)],
-    )(near_high, near_low, w_before, w_after, start, part)
+    near_high, near_low, weights, step, rest = call(
+        functools.partial(sweep_kernel, inverse, home[0], home[-1]),
+        [SMEM, VMEM, FAR, FAR, VMEM, FAR, FAR, VMEM],
+        [(near_wide, bf16, VMEM)] * 2 + [(square, f32, VMEM)] + [(square, bf16, VMEM)] * 2,
+    )(me, y, y_before, y_after, start, w_before, w_after, part)
     step_before, step_after = send(step, up), send(step, down)
-    part = call(own_step_kernel, [VMEM] * 5, [(square, f32, VMEM)])(
-        own_high, own_low, step, rest, weights
-    )
+    part = call(own_step_kernel, [FAR] * 2 + [VMEM] * 3, [(square, f32, VMEM)])(own_high, own_low, step, rest, weights)
     gain = call(
         functools.partial(gain_kernel, inverse),
-        [VMEM] * 4,
+        [FAR] * 2 + [VMEM] * 2,
         [((rows, OBS_BLOCK), bf16, VMEM)],
         [pltpu.VMEM((devices * (CAP + 1) * lines, OBS_BLOCK), f32)],
     )(arrived.reshape(-1, members), arrived, y, meta)
@@ -287,7 +309,7 @@
         coded.reshape(devices, CAP, lines, members), AXES, 0, 0, tiled=True
     ).astype(f32)
     returned = returned * jnp.abs(returned) * 256.0
-    return call(collect_kernel, [SMEM, VMEM, VMEM], [((tiles, lines, members), f32, VMEM)])(
+    return call(collect_kernel, [SMEM, VMEM, VMEM], [((tiles, lines, members), f32, FREE)])(
         slot, prior_states, returned.reshape(slots, lines, members)
     )
 

time: 104 us -> 77.7 us (0.75)
  starting transfers between devices: 40.9 us -> 24.4 us
  Pallas kernels: 27.9 us -> 16.5 us
  waiting for transfers between devices: 13.2 us -> 17 us
  other arithmetic: 2.18 us -> 0.32 us
    ppermute x11 -> x8, starting transfers between devices: 35.8 us -> 19.1 us  [send(): return lax.ppermute(values, AXES, pairs)]
    pallas_call x9 -> x8, Pallas kernels: 27.9 us -> 16.5 us  [on_chip(): run(*(pltpu.with_memory_space_constraint(operand, held[space]) if space i...]
    ppermute x11 -> x8, waiting for transfers between devices: 13.2 us -> 17 us  [send(): return lax.ppermute(values, AXES, pairs)]
    unnamed x28 -> x26, local copies, waits for them, and re-layouts: 3.97 us -> 3.16 us
  transfers between devices with their start and end apart: 12 -> 9, of which waited for: 4 -> 5; matrix products, arithmetic and copies ran while one was open for 0% -> 0% of each run, Pallas kernels for 19% -> 16%
where the time goes in v3:
time: 77.7 us; the launch traced here: 77.2 us
  starting transfers between devices  24.4 us (31%)
  waiting for transfers between devices  17 us (22%)
  Pallas kernels  16.5 us (21%)
  blocking collectives  15.6 us (20%)
  local copies, waits for them, and re-layouts  3.16 us (4%)
    ppermute x8, starting transfers between devices, send(): return lax.ppermute(values, AXES, pairs)  19.1 us
    ppermute x8, waiting for transfers between devices, send(): return lax.ppermute(values, AXES, pairs)  17 us
    pallas_call x8, Pallas kernels, on_chip(): run(*(pltpu.with_memory_space_constraint(operand, held[space]) if space i...  16.5 us
    all_to_all x1, blocking collectives, shards(): lax.all_to_all(coded.reshape(devices, CAP, lines, members), AXES, 0, 0, t...  15.6 us
    all_to_all x1, starting transfers between devices, shards(): arrived = lax.all_to_all(send_rows, AXES, 0, 0, tiled=True)  5.35 us
    unnamed x26, local copies, waits for them, and re-layouts  3.16 us
  transfers between devices with their start and end apart: 9, of which 5 were waited for; matrix products, arithmetic and copies ran while one was open for 0% of the time, Pallas kernels for 16%

profile of v3, /device:TPU:1, one launch (start us, length us, event | category | flops | bytes accessed | tf_op | source)
XLA Modules:
  0.0 77.2 jit_solution(13629019766492858308)
XLA Ops:
  0.0 0.0 copy-start.4
  0.0 0.7 copy-done.4
  0.7 0.0 copy-start.5
  0.7 0.7 copy-done.5
  1.4 0.0 copy-start.10
  1.4 0.0 copy-start.2
  1.4 0.0 copy-start.3
  1.4 0.0 copy-start.6
  1.4 0.0 copy-start.7
  1.4 1.4 %shard_map.83 = f32[520,256]{1,0:T(8,128)S(1)} custom-call(bf16[512,256]{1,0:T(8,128)(2,1)} %y_ref.1, s32[4,128]{1,0:T(4,128)S(1)} %bitcast.7, f32[4,128]{1,0:T(4,128)S(1)} %bitcast.8, f32[512,256]{1,0:T(8,128)} %target_ref.1), custom_call_target="tpu_custom_call" | custom-call | tf_op jit(solution)/shard_map/pallas_call | solution.py:229
  2.8 5.6 %collective-permute-start.3 = (f32[520,256]{1,0:T(8,128)S(1)}, f32[520,256]{1,0:T(8,128)S(1)}, u32[]{:S(2)}, u32[]{:S(2)}) collective-permute-start(f32[520,256]{1,0:T(8,128)S(1)} %shard_map.83), channel_id=1, source_target_pairs={{0,0},{1,4},{2,1},{3,5},{4,2},{5,6},{6,3},{7,7},{8,11},{9,15},{10,... | collective-permute-start | bytes 1597448 | tf_op jit(solution)/shard_map/ppermute | solution.py:261
  8.4 6.2 %collective-permute-done.3.start_ref = f32[520,256]{1,0:T(8,128)S(1)} collective-permute-done((f32[520,256]{1,0:T(8,128)S(1)}, f32[520,256]{1,0:T(8,128)S(1)}, u32[]{:S(2)}, u32[]{:S(2)}) %collective-permute-start.3) | collective-permute-done | bytes 532512 | tf_op jit(solution)/shard_map/ppermute | solution.py:261
  14.6 7.7 %collective-permute-start.4 = (f32[520,256]{1,0:T(8,128)S(1)}, f32[520,256]{1,0:T(8,128)S(1)}, u32[]{:S(2)}, u32[]{:S(2)}) collective-permute-start(f32[520,256]{1,0:T(8,128)S(1)} %collective-permute-done.3.start_ref), channel_id=1, source_target_pairs={{0,4},{4,1},{1,5},{5,2},{2,6},{6,3},{3,7},{7,11},{11,15},{15,10},{... | collective-permute-start | bytes 1597448 | tf_op jit(solution)/shard_map/ppermute | solution.py:261
  22.3 0.0 collective-permute-start.5
  22.3 0.0 copy-done.10
  22.3 2.6 %collective-permute-start = (bf16[512,256]{1,0:T(8,128)(2,1)S(1)}, bf16[512,256]{1,0:T(8,128)(2,1)S(1)}, u32[]{:S(2)}, u32[]{:S(2)}) collective-permute-start(bf16[512,256]{1,0:T(8,128)(2,1)S(1)} %copy-done.10), channel_id=1, source_target_pairs={{0,0},{1,4},{2,1},{3,5},{4,2},{5,6},{6,3},{7,7},{8,11},{9,15},{10,... | collective-permute-start | bytes 786440 | tf_op jit(solution)/shard_map/ppermute | solution.py:261
  25.0 0.0 copy-done.2
  25.0 0.0 copy-done.3
  25.0 0.0 copy-done.6
  25.0 0.0 copy-done.7
  25.0 2.9 %shard_map.82 = (bf16[32,3,8,256]{3,2,1,0:T(8,128)(2,1)}, s32[40]{0:T(128)S(1)}) custom-call(s32[32]{0:T(128)S(1)} %copy-done.7, s32[8,5]{1,0:T(8,128)S(1)} %copy-done.3, s32[8]{0:T(128)S(1)} %copy-done.6, bf16[8,8,256]{2,1,0:T(8,128)(2,1)S(1)} %copy-done.2), custom_call_target="tpu_custom_call" | custom-call | tf_op jit(solution)/shard_map/pallas_call | solution.py:229
  27.9 5.3 %all-to-all-start = ((bf16[32,3,8,256]{3,2,1,0:T(8,128)(2,1)}), bf16[32,3,8,256]{3,2,1,0:T(8,128)(2,1)}, u32[]{:S(2)}, u32[]{:S(2)}) async-start(bf16[32,3,8,256]{3,2,1,0:T(8,128)(2,1)} %get-tuple-element.25), calls=%async_computation | async-start | bytes 786432 | tf_op jit(solution)/shard_map/all_to_all | solution.py:289
  33.3 0.5 collective-permute-done.y_ref
  33.8 2.6 %collective-permute-start.1 = (bf16[512,256]{1,0:T(8,128)(2,1)S(1)}, bf16[512,256]{1,0:T(8,128)(2,1)S(1)}, u32[]{:S(2)}, u32[]{:S(2)}) collective-permute-start(bf16[512,256]{1,0:T(8,128)(2,1)S(1)} %collective-permute-done.y_ref), channel_id=1, source_target_pairs={{0,4},{4,1},{1,5},{5,2},{2,6},{6,3},{3,7},{7,11},{11,15},{15,10},{... | collective-permute-start | bytes 786440 | tf_op jit(solution)/shard_map/ppermute | solution.py:261
  36.5 0.0 collective-permute-start.2
  36.5 1.7 %shard_map.84 = (bf16[512,512]{1,0:T(8,128)(2,1)}, bf16[512,512]{1,0:T(8,128)(2,1)}, f32[512,256]{1,0:T(8,128)S(1)}, f32[8,256]{1,0:T(8,128)S(1)}) custom-call(bf16[512,256]{1,0:T(8,128)(2,1)S(1)} %collective-permute-done.y_ref, f32[520,256]{1,0:T(8,128)S(1)} %collective-permute-done.3.start_ref), custom_call_target="tpu_custom_call" | custom-call | tf_op jit(solution)/shard_map/pallas_call | solution.py:229
  38.2 4.8 %collective-permute-done.1.y_before_ref = bf16[512,256]{1,0:T(8,128)(2,1)S(1)} collective-permute-done((bf16[512,256]{1,0:T(8,128)(2,1)S(1)}, bf16[512,256]{1,0:T(8,128)(2,1)S(1)}, u32[]{:S(2)}, u32[]{:S(2)}) %collective-permute-start.1) | collective-permute-done | bytes 262176 | tf_op jit(solution)/shard_map/ppermute | solution.py:261
  43.0 0.0 copy-start.11
  43.0 2.3 %collective-permute-done.2.y_after_ref = bf16[512,256]{1,0:T(8,128)(2,1)S(1)} collective-permute-done((bf16[512,256]{1,0:T(8,128)(2,1)S(1)}, bf16[512,256]{1,0:T(8,128)(2,1)S(1)}, u32[]{:S(2)}, u32[]{:S(2)}) %collective-permute-start.2) | collective-permute-done | bytes 262176 | tf_op jit(solution)/shard_map/ppermute | solution.py:261
  45.3 0.0 copy-start.12
  45.3 0.0 collective-permute-done.4.before_ref
  45.3 0.0 copy-start.8
  45.3 0.0 collective-permute-done.5.after_ref
  45.3 0.0 copy-start.9
  45.3 0.0 copy-done.11
  45.4 0.7 copy-done.12
  46.0 0.2 copy-done.8
  46.2 0.2 copy-done.9
  46.4 4.2 %shard_map.85 = (bf16[512,1024]{1,0:T(8,128)(2,1)S(1)}, bf16[512,1024]{1,0:T(8,128)(2,1)S(1)}, f32[512,256]{1,0:T(8,128)S(1)}, bf16[512,256]{1,0:T(8,128)(2,1)}, bf16[512,256]{1,0:T(8,128)(2,1)S(1)}) custom-call(s32[1]{0:T(128)} %bitcast.me_ref, bf16[512,256]{1,0:T(8,128)(2,1)S(1)} %collective-permute-done.y_ref, bf16[512,256]{1,0:T(8,128)(2,1)} %copy-done.11, ...), custom_call_target="tpu_custom_call" | custom-call | tf_op jit(solution)/shard_map/pallas_call | solution.py:229
  50.7 0.0 copy-start
  50.7 0.7 copy-done
  51.4 0.2 collective-permute-start.6
  51.6 0.3 collective-permute-start.7
  51.9 0.0 all-to-all-done.slabs_ref
  51.9 0.0 copy-start.1
  51.9 1.9 %shard_map.87.gain_ref = bf16[512,512]{1,0:T(8,128)(2,1)S(1)} custom-call(bf16[768,256]{1,0:T(8,128)(2,1)} %bitcast.3.rows_ref, bf16[32,3,8,256]{3,2,1,0:T(8,128)(2,1)} %all-to-all-done.slabs_ref, bf16[512,256]{1,0:T(8,128)(2,1)S(1)} %collective-permute-done.y_ref, f32[8,256]{1,0:T(8,128)S(1)} %get-tuple-element.26.meta_ref), custom_call_target="tpu_custom_call" | custom-call | tf_op jit(solution)/shard_map/pallas_call | solution.py:229
  53.8 0.0 copy-done.1
  53.8 1.8 %shard_map.86.part_ref = f32[512,256]{1,0:T(8,128)S(1)} custom-call(bf16[512,512]{1,0:T(8,128)(2,1)} %get-tuple-element.21.high_ref, bf16[512,512]{1,0:T(8,128)(2,1)} %get-tuple-element.22.low_ref, bf16[512,256]{1,0:T(8,128)(2,1)} %get-tuple-element.20.step_ref, bf16[512,256]{1,0:T(8,128)(2,1)S(1)} %copy-done.1, f32[512,256]{1,0:T(8,128)S(1)} %get-tuple-element.24.weights_ref), custom_call_target="tpu_custom_call" | custom-call | tf_op jit(solution)/shard_map/pallas_call | solution.py:229
  55.7 0.0 collective-permute-done.6.before_ref
  55.7 3.1 %collective-permute-done.7.after_ref = bf16[512,256]{1,0:T(8,128)(2,1)S(1)} collective-permute-done((bf16[512,256]{1,0:T(8,128)(2,1)}, bf16[512,256]{1,0:T(8,128)(2,1)S(1)}, u32[]{:S(2)}, u32[]{:S(2)}) %collective-permute-start.7) | collective-permute-done | bytes 262176 | tf_op jit(solution)/shard_map/ppermute | solution.py:261
  58.8 1.2 %shard_map.88 = f32[512,256]{1,0:T(8,128)S(1)} custom-call(bf16[512,1024]{1,0:T(8,128)(2,1)S(1)} %get-tuple-element.18.high_ref, bf16[512,1024]{1,0:T(8,128)(2,1)S(1)} %get-tuple-element.19.low_ref, bf16[512,256]{1,0:T(8,128)(2,1)S(1)} %collective-permute-done.6.before_ref, bf16[512,256]{1,0:T(8,128)(2,1)S(1)} %collective-permute-done.7.after_ref, ...), custom_call_target="tpu_custom_call" | custom-call | tf_op jit(solution)/shard_map/pallas_call | solution.py:229
  60.0 0.2 fusion
  60.2 15.6 %all_to_all.10 = f16[32,2,8,256]{3,2,1,0:T(8,128)(2,1)S(1)} all-to-all(f16[32,2,8,256]{3,2,1,0:T(8,128)(2,1)S(1)} %bitcast.9), channel_id=1, replica_groups=mesh['atm'=8,'ocn'=4] {'atm','ocn'}, dimensions={0} | all-to-all | bytes 524288 | tf_op jit(solution)/shard_map/all_to_all | solution.py:308
  75.8 0.1 fusion.1
  75.9 1.3 %shard_map.89 = f32[8,8,256]{2,1,0:T(8,128)} custom-call(s32[40]{0:T(128)S(1)} %get-tuple-element.16.slot_ref, bf16[8,8,256]{2,1,0:T(8,128)(2,1)S(1)} %copy-done.2, f32[64,8,256]{2,1,0:T(8,128)S(1)} %bitcast.6), custom_call_target="tpu_custom_call" | custom-call | tf_op jit(solution)/shard_map/pallas_call | solution.py:229
Async XLA Ops:
  0.0 0.7 copy-start.4
  0.7 0.7 copy-start.5
  1.4 21.0 %copy-start.10 = (bf16[512,256]{1,0:T(8,128)(2,1)S(1)}, bf16[512,256]{1,0:T(8,128)(2,1)}, u32[]{:S(2)}) copy-start(bf16[512,256]{1,0:T(8,128)(2,1)} %y_ref.1) | copy-start | bytes 786436
  1.4 23.6 %copy-start.2 = (bf16[8,8,256]{2,1,0:T(8,128)(2,1)S(1)}, bf16[8,8,256]{2,1,0:T(8,128)(2,1)}, u32[]{:S(2)}) copy-start(bf16[8,8,256]{2,1,0:T(8,128)(2,1)} %prior_ref.3) | copy-start | bytes 98308
  1.4 23.6 %copy-start.3 = (s32[8,5]{1,0:T(8,128)S(1)}, s32[8,5]{1,0:T(8,128)}, u32[]{:S(2)}) copy-start(s32[8,5]{1,0:T(8,128)} %reads_ref.1) | copy-start | bytes 484
  1.4 23.6 %copy-start.6 = (s32[8]{0:T(128)S(1)}, s32[8]{0:T(128)}, u32[]{:S(2)}) copy-start(s32[8]{0:T(128)} %place_ref.1) | copy-start | bytes 100
  1.4 23.6 %copy-start.7 = (s32[32]{0:T(128)S(1)}, s32[32]{0:T(128)}, u32[]{:S(2)}) copy-start(s32[32]{0:T(128)} %constant.19.clone.home_ref) | copy-start | bytes 388
  2.8 11.8 %collective-permute-start.3 = (f32[520,256]{1,0:T(8,128)S(1)}, f32[520,256]{1,0:T(8,128)S(1)}, u32[]{:S(2)}, u32[]{:S(2)}) collective-permute-start(f32[520,256]{1,0:T(8,128)S(1)} %shard_map.83), channel_id=1, source_target_pairs={{0,0},{1,4},{2,1},{3,5},{4,2},{5,6},{6,3},{7,7},{8,11},{9,15},{10,... | collective-permute-start | bytes 1597448 | tf_op jit(solution)/shard_map/ppermute | solution.py:261
  14.6 30.7 %collective-permute-start.4 = (f32[520,256]{1,0:T(8,128)S(1)}, f32[520,256]{1,0:T(8,128)S(1)}, u32[]{:S(2)}, u32[]{:S(2)}) collective-permute-start(f32[520,256]{1,0:T(8,128)S(1)} %collective-permute-done.3.start_ref), channel_id=1, source_target_pairs={{0,4},{4,1},{1,5},{5,2},{2,6},{6,3},{3,7},{7,11},{11,15},{15,10},{... | collective-permute-start | bytes 1597448 | tf_op jit(solution)/shard_map/ppermute | solution.py:261
  22.3 23.0 %collective-permute-start.5 = (f32[520,256]{1,0:T(8,128)S(1)}, f32[520,256]{1,0:T(8,128)S(1)}, u32[]{:S(2)}, u32[]{:S(2)}) collective-permute-start(f32[520,256]{1,0:T(8,128)S(1)} %collective-permute-done.3.start_ref), channel_id=1, source_target_pairs={{0,28},{4,0},{1,4},{5,1},{2,5},{6,2},{3,6},{7,3},{11,7},{15,11},{1... | collective-permute-start | bytes 1597448 | tf_op jit(solution)/shard_map/ppermute | solution.py:261
  22.3 11.5 %collective-permute-start = (bf16[512,256]{1,0:T(8,128)(2,1)S(1)}, bf16[512,256]{1,0:T(8,128)(2,1)S(1)}, u32[]{:S(2)}, u32[]{:S(2)}) collective-permute-start(bf16[512,256]{1,0:T(8,128)(2,1)S(1)} %copy-done.10), channel_id=1, source_target_pairs={{0,0},{1,4},{2,1},{3,5},{4,2},{5,6},{6,3},{7,7},{8,11},{9,15},{10,... | collective-permute-start | bytes 786440 | tf_op jit(solution)/shard_map/ppermute | solution.py:261
  27.9 23.9 %all-to-all-start = ((bf16[32,3,8,256]{3,2,1,0:T(8,128)(2,1)}), bf16[32,3,8,256]{3,2,1,0:T(8,128)(2,1)}, u32[]{:S(2)}, u32[]{:S(2)}) async-start(bf16[32,3,8,256]{3,2,1,0:T(8,128)(2,1)} %get-tuple-element.25), calls=%async_computation | async-start | bytes 786432 | tf_op jit(solution)/shard_map/all_to_all | solution.py:289
  33.8 9.1 %collective-permute-start.1 = (bf16[512,256]{1,0:T(8,128)(2,1)S(1)}, bf16[512,256]{1,0:T(8,128)(2,1)S(1)}, u32[]{:S(2)}, u32[]{:S(2)}) collective-permute-start(bf16[512,256]{1,0:T(8,128)(2,1)S(1)} %collective-permute-done.y_ref), channel_id=1, source_target_pairs={{0,4},{4,1},{1,5},{5,2},{2,6},{6,3},{3,7},{7,11},{11,15},{15,10},{... | collective-permute-start | bytes 786440 | tf_op jit(solution)/shard_map/ppermute | solution.py:261
  36.5 8.8 %collective-permute-start.2 = (bf16[512,256]{1,0:T(8,128)(2,1)S(1)}, bf16[512,256]{1,0:T(8,128)(2,1)S(1)}, u32[]{:S(2)}, u32[]{:S(2)}) collective-permute-start(bf16[512,256]{1,0:T(8,128)(2,1)S(1)} %collective-permute-done.y_ref), channel_id=1, source_target_pairs={{0,28},{4,0},{1,4},{5,1},{2,5},{6,2},{3,6},{7,3},{11,7},{15,11},{1... | collective-permute-start | bytes 786440 | tf_op jit(solution)/shard_map/ppermute | solution.py:261
  43.0 2.4 %copy-start.11 = (bf16[512,256]{1,0:T(8,128)(2,1)}, bf16[512,256]{1,0:T(8,128)(2,1)S(1)}, u32[]{:S(2)}) copy-start(bf16[512,256]{1,0:T(8,128)(2,1)S(1)} %collective-permute-done.1.y_before_ref) | copy-start | bytes 786436
  45.3 0.7 copy-start.12
  45.3 0.9 %copy-start.8 = (f32[520,256]{1,0:T(8,128)}, f32[520,256]{1,0:T(8,128)S(1)}, u32[]{:S(2)}) copy-start(f32[520,256]{1,0:T(8,128)S(1)} %collective-permute-done.4.before_ref) | copy-start | bytes 1597444
  45.3 1.1 %copy-start.9 = (f32[520,256]{1,0:T(8,128)}, f32[520,256]{1,0:T(8,128)S(1)}, u32[]{:S(2)}) copy-start(f32[520,256]{1,0:T(8,128)S(1)} %collective-permute-done.5.after_ref) | copy-start | bytes 1597444
  50.7 0.7 copy-start
  51.4 4.3 %collective-permute-start.6 = (bf16[512,256]{1,0:T(8,128)(2,1)}, bf16[512,256]{1,0:T(8,128)(2,1)S(1)}, u32[]{:S(2)}, u32[]{:S(2)}) collective-permute-start(bf16[512,256]{1,0:T(8,128)(2,1)} %get-tuple-element.20.step_ref), channel_id=1, source_target_pairs={{0,4},{4,1},{1,5},{5,2},{2,6},{6,3},{3,7},{7,11},{11,15},{15,10},{... | collective-permute-start | bytes 786440 | tf_op jit(solution)/shard_map/ppermute | solution.py:261
  51.6 7.2 %collective-permute-start.7 = (bf16[512,256]{1,0:T(8,128)(2,1)}, bf16[512,256]{1,0:T(8,128)(2,1)S(1)}, u32[]{:S(2)}, u32[]{:S(2)}) collective-permute-start(bf16[512,256]{1,0:T(8,128)(2,1)} %get-tuple-element.20.step_ref), channel_id=1, source_target_pairs={{0,28},{4,0},{1,4},{5,1},{2,5},{6,2},{3,6},{7,3},{11,7},{15,11},{1... | collective-permute-start | bytes 786440 | tf_op jit(solution)/shard_map/ppermute | solution.py:261
  51.9 1.9 %copy-start.1 = (bf16[512,256]{1,0:T(8,128)(2,1)S(1)}, bf16[512,256]{1,0:T(8,128)(2,1)}, u32[]{:S(2)}) copy-start(bf16[512,256]{1,0:T(8,128)(2,1)} %copy-done) | copy-start | bytes 786436
